TPU v7x, 32 devices: a whole 2x2x4 slice. The times are simulated.
32 devices in a mesh: group: 2 (over x), seq: 8 (over z, y), clip: 2 (over core).
Axes of the slice: x: 2, y: 2, z: 4, core: 2. Of those that a mesh axis runs over, the one named last changes fastest.
Arguments:
- latent: float32 [4, 8, 256, 128], P(('group', 'clip'), 'seq'), parts along dimension 0, may hold values from -6 to 6
- context: float32 [4, 8, 256, 128], P(('group', 'clip'), 'seq'), parts along dimension 0, may hold values from -6 to 6
- frozen: int32 [16], P('group'), parts along dimension 0, may hold values 0 or 1
- read_list: int32 [16, 3], P('group'), parts along dimension 0, may hold values from -1 to 6, as said below
- w_embed: bfloat16 [128, 1536], replicated, may hold values from -0.5 to 0.5
- w_qkv: bfloat16 [3, 1536, 1536], P(None, None, 'clip')
- w_attn_out: bfloat16 [1536, 1536], P('clip'), may hold values from -0.45898438 to 0.45898438
- w_head: bfloat16 [1536, 256], replicated, may hold values from -0.15625 to 0.15625
Outputs:
- mirrored: float32 [4, 8, 256, 128], P(('group', 'clip'), 'seq'), parts along dimension 0
There are 2 independent parts, one for each index of `group`. A program takes and returns all parts, laid end to end along the dimension named above; an argument that names none is the same for every part. Nothing has to cross between parts.
Inputs may be any that keep to these rules, and one draw needn't show every extreme that they name: `read_list`: row f lists min(f, 3) distinct earlier frames, the first of them f - 1, and -1 in the remaining entries.
All inputs are finite; a program needn't handle non-finite values.
Results may differ from a plain program's by a relative error of at most 0.015.
Values may be sent and summed in bfloat16 or wider, within the bound.
No kernel may reach another device: no remote copies, remote signals or barrier semaphores. Data moves between devices by JAX's collectives and lax.ppermute only.
A program may use at most 128 MiB of HBM per device.

v0:
```python
import functools
import math

import jax
import jax.numpy as jnp
from jax import lax
from jax.experimental import pallas as pl
from jax.experimental.pallas import tpu as pltpu
from jax.sharding import PartitionSpec as P


HD = 128
EPSILON = 1e-05
F32 = jnp.float32
BF16 = jnp.bfloat16


def split_bf16(value, pieces):
    out = []
    for _ in range(pieces):
        piece = value.astype(BF16)
        out.append(piece)
        value = value - piece.astype(F32)
    return out


def fold_kernel(embed_ref, qkv_hbm, folded_ref, gram_ref, qkv, centred_ref, sems):
    channels, width = embed_ref.shape
    pairs = folded_ref.shape[0]
    loads = [pltpu.make_async_copy(qkv_hbm.at[index], qkv.at[index], sems.at[index]) for index in range(3)]
    for load in loads:
        load.start()

    rows = embed_ref[...].astype(F32)
    centred = rows - jnp.mean(rows, axis=1, keepdims=True)
    high, low = split_bf16(centred, 2)
    centred_ref[:channels] = high
    centred_ref[channels:] = low
    square = lax.dot_general(
        centred_ref[...], centred_ref[...], (((1,), (1,)), ((), ())), preferred_element_type=F32
    )
    gram = (
        square[:channels, :channels] + square[channels:, channels:]
        + square[:channels, channels:] + square[channels:, :channels]
    ) * (1.0 / width)
    for index, piece in enumerate(split_bf16(gram, 3)):
        gram_ref[:, index * channels:(index + 1) * channels] = piece

    scale = math.log2(math.e) / math.sqrt(HD)
    maps = []
    for index in range(3):
        loads[index].wait()
        product = jnp.dot(centred_ref[...], qkv[index], preferred_element_type=F32)
        maps.append(product[:channels] + product[channels:])
        if index == 1:
            for head in range(2 * pairs):
                cols = slice(head * HD, (head + 1) * HD)
                queries = split_bf16(maps[0][:, cols] * scale, 2)
                keys = split_bf16(maps[1][:, cols], 2)
                score_map = lax.dot_general(
                    jnp.concatenate([keys[0], keys[0]], axis=1), jnp.concatenate(queries, axis=1),
                    (((1,), (1,)), ((), ())), preferred_element_type=F32,
                ) + lax.dot_general(
                    keys[1], queries[0], (((1,), (1,)), ((), ())), preferred_element_type=F32
                )
                half = head % 2 * HD
                folded_ref[head // 2, half:half + HD, :channels] = score_map.astype(BF16)
    for head in range(2 * pairs):
        half = head % 2 * HD
        mixed = maps[2][:, head * HD:(head + 1) * HD].T.astype(BF16)
        blank = jnp.zeros((HD, channels), BF16)
        folded_ref[head // 2, half:half + HD, channels:] = jnp.concatenate(
            [blank, mixed] if head % 2 else [mixed, blank], axis=1
        )


def fold_weights(w_embed, w_qkv):
    channels, width = w_embed.shape
    cols = w_qkv.shape[2]
    wide = 2 * HD
    pairs = cols // wide
    vmem = pl.BlockSpec(memory_space=pltpu.VMEM)
    return pl.pallas_call(
        fold_kernel,
        in_specs=[vmem, pl.BlockSpec(memory_space=pl.ANY)],
        out_specs=[vmem, vmem],
        out_shape=[
            jax.ShapeDtypeStruct((pairs, wide, channels + wide), BF16),
            jax.ShapeDtypeStruct((channels, 3 * channels), BF16),
        ],
        scratch_shapes=[
            pltpu.VMEM((3, width, cols), BF16),
            pltpu.VMEM((2 * channels, width), BF16),
            pltpu.SemaphoreType.DMA((3,)),
        ],
        compiler_params=pltpu.CompilerParams(vmem_limit_bytes=67043328),
        cost_estimate=pl.CostEstimate(
            flops=4 * channels * width * 3 * cols, bytes_accessed=6 * width * cols, transcendentals=0
        ),
        name="fold",
    )(w_embed, w_qkv)


def flow_kernel(counts, place_ref, frozen_ref, read_ref, gram_hbm, embed_hbm, head_hbm, *rest):
    frames, parts = counts
    block_hbm, rest = rest[:frames], rest[frames:]
    folded_hbm, out_hbm, rest = rest[:parts], rest[parts:2 * parts], rest[2 * parts:]
    (result_ref, raw, turned, straight, query, keys, values, mapped, attended,
     folded, w_out, w_head, gram_ref, ready, sems) = rest
    tokens, channels = raw.shape[1:]
    links = read_ref.shape[0]
    slots = links + 1
    pairs_here = folded_hbm[0].shape[0]
    rows_here = out_hbm[0].shape[0]
    hidden = parts * rows_here
    place = place_ref[0]

    block_loads = [
        pltpu.make_async_copy(block_hbm[slot], raw.at[slot], sems.at[slot]) for slot in range(frames)
    ]
    block_loads.append(pltpu.make_async_copy(gram_hbm, gram_ref, sems.at[frames + 2 * parts + 2]))
    folded_loads, late_loads = [], []
    for part in range(parts):
        folded_loads.append(pltpu.make_async_copy(
            folded_hbm[part], folded.at[part * pairs_here:(part + 1) * pairs_here], sems.at[frames + part]))
        late_loads.append(pltpu.make_async_copy(
            out_hbm[part], w_out.at[part * rows_here:(part + 1) * rows_here], sems.at[frames + parts + part]))
    late_loads.append(pltpu.make_async_copy(embed_hbm, w_out.at[hidden:], sems.at[frames + 2 * parts]))
    late_loads.append(pltpu.make_async_copy(head_hbm, w_head, sems.at[frames + 2 * parts + 1]))
    for load in block_loads + folded_loads + late_loads:
        load.start()
    ready[0] = 0

    def await_late():
        @pl.when(ready[0] == 0)
        def _():
            for load in late_loads:
                load.wait()
            ready[0] = 1

    def slot_of(frame):
        return jnp.bitwise_xor(place, frame)

    def ingest(slot, rounded):
        wide = rounded.astype(F32)
        spread = jnp.dot(rounded, gram_ref[...], preferred_element_type=F32)
        spread = spread[:, :channels] + spread[:, channels:2 * channels] + spread[:, 2 * channels:]
        variance = jnp.maximum(jnp.sum(spread * wide, axis=1, keepdims=True), 0.0)
        scaled = (wide * lax.rsqrt(variance + EPSILON)).astype(BF16)
        straight[slot] = scaled
        turned[slot, :channels] = scaled.T
        turned[slot, channels:] = jnp.ones((turned.shape[1] - channels, tokens), BF16)

    for load in block_loads:
        load.wait()
    group = math.gcd(frames, 4)

    def ingest_step(index, carry):
        for side in range(group):
            slot = index * group + side
            ingest(slot, raw[slot])
        return carry

    lax.fori_loop(0, frames // group, ingest_step, 0)
    for load in folded_loads:
        load.wait()

    target = frames - 1 - place
    last = target - 1
    last_safe = jnp.maximum(last, 0)
    run_all = jnp.logical_and(target > 0, frozen_ref[target] == 0)

    def flip():
        rows = lax.broadcasted_iota(jnp.int32, (tokens, tokens), 0)
        cols = lax.broadcasted_iota(jnp.int32, (tokens, tokens), 1)
        return jnp.where(rows + cols == tokens - 1, 1.0, 0.0).astype(BF16)

    def source_of(index):
        return jnp.where(index == 0, last_safe, read_ref[jnp.maximum(index - 1, 0), last_safe])

    def is_run(index):
        frame = source_of(index)
        return jnp.logical_and(frame > 0, frozen_ref[jnp.maximum(frame, 0)] == 0)

    def scores_of(pair, side):
        return jnp.dot(keys[...], mapped[pair, side * HD:(side + 1) * HD], preferred_element_type=F32)

    def context_of(exponents):
        weights = jnp.exp2(exponents).astype(BF16)
        total = jnp.dot(values[...], weights, preferred_element_type=F32)
        mass = total[channels:channels + 1]
        return (total[:channels] / mass).astype(BF16), mass

    def mix(pair, contexts):
        mixed = jnp.dot(
            folded[pair, :, channels:], jnp.concatenate(contexts, axis=0), preferred_element_type=F32
        )
        return mixed.astype(BF16).T

    def attend():
        heads = 2 * folded.shape[0]
        scores, contexts = scores_of(0, 0), []
        fits = jnp.ones((1, tokens), F32)
        for head in range(heads):
            following = scores_of((head + 1) // 2, (head + 1) % 2) if head + 1 < heads else None
            context, mass = context_of(scores)
            fits = jnp.where(jnp.logical_and(mass > 2.0 ** -80, mass < 2.0 ** 110), fits, 0.0)
            contexts.append(context)
            scores = following
            if head % 2:
                pair = head // 2
                attended[:, pair * 2 * HD:(pair + 1) * 2 * HD] = mix(pair, contexts)
                contexts = []

        @pl.when(jnp.min(fits) < 0.5)
        def _():
            def shifted_pair(pair, carry):
                contexts = []
                for side in range(2):
                    scores = scores_of(pair, side)
                    contexts.append(context_of(scores - jnp.max(scores, axis=0, keepdims=True))[0])
                start = pl.multiple_of(pair * 2 * HD, 2 * HD)
                attended[:, pl.ds(start, 2 * HD)] = mix(pair, contexts)
                return carry

            lax.fori_loop(0, folded.shape[0], shifted_pair, 0)

    def evaluate():
        for pair in range(folded.shape[0]):
            mapped[pair] = jnp.dot(
                folded[pair, :, :channels], query[...], preferred_element_type=F32
            ).astype(BF16)
        attend()
        await_late()
        residual = jnp.dot(attended[...], w_out[...], preferred_element_type=F32)
        centred = residual - jnp.mean(residual, axis=1, keepdims=True)
        spread_sq = jnp.mean(centred * centred, axis=1, keepdims=True)
        head_in = (centred * lax.rsqrt(spread_sq + EPSILON)).astype(BF16)
        return jnp.dot(head_in, w_head[...], preferred_element_type=F32)

    def moved(held, predicted):
        return held * jnp.exp(jnp.tanh(predicted[:, channels:])) + predicted[:, :channels]

    def place_key(index, slot, usable):
        keys[index * tokens:(index + 1) * tokens] = straight[slot]
        block = turned[slot]
        values[:, index * tokens:(index + 1) * tokens] = jnp.where(usable, block, jnp.zeros_like(block))

    def round_step(step, carry):
        final = step == slots

        @pl.when(jnp.logical_and(run_all, jnp.logical_or(final, is_run(jnp.minimum(step, slots - 1)))))
        def _():
            frame = jnp.where(final, last_safe, source_of(jnp.minimum(step, slots - 1)) - 1)
            frame = jnp.maximum(frame, 0)
            own = jnp.where(jnp.logical_and(final, is_run(0)), frames, slot_of(frame))
            attended[:, hidden:] = raw[own]
            query[...] = turned[own, :channels]
            place_key(0, own, True)
            for link in range(links):
                source = read_ref[link, frame]
                usable = source >= 0
                held = slot_of(jnp.maximum(source, 0))
                held = jnp.where(jnp.logical_and(final, is_run(link + 1)), frames + link + 1, held)
                place_key(link + 1, jnp.where(usable, held, own), usable)

            @pl.when(final)
            def _():
                mirror = flip()
                attended[:, hidden:] = jnp.dot(mirror, raw[own], preferred_element_type=F32).astype(BF16)
                query[...] = jnp.dot(query[...], mirror, preferred_element_type=F32).astype(BF16)

            predicted = evaluate()

            @pl.when(jnp.logical_not(final))
            def _():
                base = raw[slot_of(frame + 1)].astype(F32)
                rounded = moved(base, predicted).astype(BF16)
                raw[frames + step] = rounded
                ingest(frames + step, rounded)

            @pl.when(final)
            def _():
                base = jnp.dot(flip(), raw[slot_of(target)], preferred_element_type=F32)
                result_ref[...] = moved(base, predicted)

        return carry

    lax.fori_loop(0, slots + 1, round_step, 0)
    await_late()

    @pl.when(jnp.logical_not(run_all))
    def _():
        result_ref[...] = jnp.dot(flip(), raw[slot_of(target)], preferred_element_type=F32)


def run_flow(place, frozen, read_list, blocks, gram, w_embed, w_head, folded, outs):
    tokens, channels = blocks[0].shape
    frames = len(blocks)
    parts = len(folded)
    slots = read_list.shape[0] + 1
    width = w_embed.shape[1]
    pairs = sum(block.shape[0] for block in folded)
    hidden = sum(block.shape[0] for block in outs)
    vmem = pl.BlockSpec(memory_space=pltpu.VMEM)
    smem = pl.BlockSpec(memory_space=pltpu.SMEM)
    anywhere = pl.BlockSpec(memory_space=pl.ANY)
    held = frames + slots
    return pl.pallas_call(
        functools.partial(flow_kernel, (frames, parts)),
        in_specs=[smem, smem, smem] + [anywhere] * (3 + frames + 2 * parts),
        out_specs=vmem,
        out_shape=jax.ShapeDtypeStruct((tokens, channels), F32),
        scratch_shapes=[
            pltpu.VMEM((held, tokens, channels), BF16),
            pltpu.VMEM((held, channels + 16, tokens), BF16),
            pltpu.VMEM((held, tokens, channels), BF16),
            pltpu.VMEM((channels, tokens), BF16),
            pltpu.VMEM((slots * tokens, channels), BF16),
            pltpu.VMEM((channels + 16, slots * tokens), BF16),
            pltpu.VMEM((pairs, 2 * HD, tokens), BF16),
            pltpu.VMEM((tokens, hidden + channels), BF16),
            pltpu.VMEM((pairs,) + folded[0].shape[1:], BF16),
            pltpu.VMEM((hidden + channels, width), BF16),
            pltpu.VMEM(w_head.shape, BF16),
            pltpu.VMEM(gram.shape, BF16),
            pltpu.SMEM((1,), jnp.int32),
            pltpu.SemaphoreType.DMA((frames + 3 + 2 * parts,)),
        ],
        compiler_params=pltpu.CompilerParams(vmem_limit_bytes=67043328),
        name="flow",
    )(place, frozen, read_list, gram, w_embed, w_head, *blocks, *folded, *outs)


def from_behind(value, axis, shift):
    count = lax.axis_size(axis)
    return lax.ppermute(value, axis, [(source, (source + shift) % count) for source in range(count)])


def across(value, axis, mask):
    return lax.ppermute(value, axis, [(source, source ^ mask) for source in range(lax.axis_size(axis))])


def per_device(latent, context, frozen, read_list, w_embed, w_qkv, w_attn_out, w_head):
    position = lax.axis_index("seq")
    seq_count = lax.axis_size("seq")
    clip_count = lax.axis_size("clip")
    layout = latent.shape
    frozen_here = lax.dynamic_index_in_dim(frozen, position, 0, keepdims=False) == 1
    held = jnp.where(frozen_here, context, latent).astype(BF16).reshape(layout[-2], layout[-1])
    blocks = [None] * seq_count
    blocks[0] = held
    for mask in [1] + list(range(2, seq_count, 2)):
        blocks[mask] = across(held, "seq", mask)
    for mask in range(2, seq_count, 2):
        blocks[mask + 1] = across(blocks[mask], "seq", 1)
    outs = [w_attn_out] + [from_behind(w_attn_out, "clip", step) for step in range(1, clip_count)]
    folded, gram = fold_weights(w_embed, w_qkv)
    folded = [folded] + [from_behind(folded, "clip", step) for step in range(1, clip_count)]
    result = run_flow(
        position.reshape(1).astype(jnp.int32), frozen, read_list.T, blocks, gram, w_embed, w_head, folded, outs
    )
    return result.reshape(layout)


def solution(mesh):
    return jax.shard_map(
        per_device,
        mesh=mesh,
        in_specs=(
            P(("group", "clip"), "seq", None, None),
            P(("group", "clip"), "seq", None, None),
            P("group"),
            P("group", None),
            P(),
            P(None, None, "clip"),
            P("clip", None),
            P(),
        ),
        out_specs=P(("group", "clip"), "seq", None, None),
        check_vma=False,
    )
```

profile of v0, /device:TPU:10, one launch (start us, length us, event | category | flops | bytes accessed | tf_op | source)
XLA Modules:
  0.0 98.8 jit_solution(5597247617291888879)
XLA Ops:
  0.0 0.0 collective-permute-start.8
  0.0 6.6 %fold.1 = (bf16[3,256,384]{2,1,0:T(8,128)(2,1)}, bf16[128,384]{1,0:T(8,128)(2,1)}) custom-call(bf16[128,1536]{1,0:T(8,128)(2,1)} %embed_hbm.1, bf16[3,1536,768]{2,1,0:T(8,128)(2,1)} %qkv_hbm.1), custom_call_target="tpu_custom_call" | custom-call | flops 1811939328 | bytes 7077888 | tf_op jit(solution)/shard_map/fold/pallas_call | solution.py:83
  6.6 0.6 collective-permute-start.7
  7.2 1.2 %dynamic_slice.4 = s32[1]{0:T(128)} dynamic-slice(s32[8]{0:T(128)} %frozen_ref.1, s32[]{:T(128)S(6)} %select_n.12), dynamic_slice_sizes={1} | dynamic-slice | bytes 12 | tf_op jit(solution)/shard_map/jit(dynamic_index_in_dim)/dynamic_slice | solution.py:349
  9.1 0.9 fusion.rest_0_
  10.0 0.0 copy-start
  10.0 1.6 %collective-permute-start.5 = (bf16[256,128]{1,0:T(8,128)(2,1)S(1)}, bf16[256,128]{1,0:T(8,128)(2,1)S(1)}, u32[]{:S(2)}, u32[]{:S(2)}) collective-permute-start(bf16[256,128]{1,0:T(8,128)(2,1)S(1)} %fusion.rest_0_), channel_id=1, source_target_pairs={{0,12},{2,14},{4,8},{6,10},{8,4},{10,6},{12,0},{14,2},{1,13},{3,15... | collective-permute-start | bytes 196616 | tf_op jit(solution)/shard_map/ppermute | solution.py:341
  11.6 1.2 %collective-permute-start.3 = (bf16[256,128]{1,0:T(8,128)(2,1)S(1)}, bf16[256,128]{1,0:T(8,128)(2,1)S(1)}, u32[]{:S(2)}, u32[]{:S(2)}) collective-permute-start(bf16[256,128]{1,0:T(8,128)(2,1)S(1)} %fusion.rest_0_), channel_id=1, source_target_pairs={{0,8},{2,10},{4,12},{6,14},{8,0},{10,2},{12,4},{14,6},{1,9},{3,11}... | collective-permute-start | bytes 196616 | tf_op jit(solution)/shard_map/ppermute | solution.py:341
  12.9 1.2 %collective-permute-start.1 = (bf16[256,128]{1,0:T(8,128)(2,1)S(1)}, bf16[256,128]{1,0:T(8,128)(2,1)S(1)}, u32[]{:S(2)}, u32[]{:S(2)}) collective-permute-start(bf16[256,128]{1,0:T(8,128)(2,1)S(1)} %fusion.rest_0_), channel_id=1, source_target_pairs={{0,4},{2,6},{4,0},{6,2},{8,12},{10,14},{12,8},{14,10},{1,5},{3,7},... | collective-permute-start | bytes 196616 | tf_op jit(solution)/shard_map/ppermute | solution.py:341
  14.1 3.4 %collective-permute-done.5.rest_6_ = bf16[256,128]{1,0:T(8,128)(2,1)S(1)} collective-permute-done((bf16[256,128]{1,0:T(8,128)(2,1)S(1)}, bf16[256,128]{1,0:T(8,128)(2,1)S(1)}, u32[]{:S(2)}, u32[]{:S(2)}) %collective-permute-start.5) | collective-permute-done | bytes 65568 | tf_op jit(solution)/shard_map/ppermute | solution.py:341
  17.5 0.0 copy-done
  17.5 0.0 copy-start.1
  17.5 1.5 %collective-permute-start = (bf16[256,128]{1,0:T(8,128)(2,1)S(1)}, bf16[256,128]{1,0:T(8,128)(2,1)S(1)}, u32[]{:S(2)}, u32[]{:S(2)}) collective-permute-start(bf16[256,128]{1,0:T(8,128)(2,1)S(1)} %fusion.rest_0_), channel_id=1, source_target_pairs={{0,2},{2,0},{4,6},{6,4},{8,10},{10,8},{12,14},{14,12},{1,3},{3,1},... | collective-permute-start | bytes 196616 | tf_op jit(solution)/shard_map/ppermute | solution.py:341
  19.0 0.0 collective-permute-done.3.rest_4_
  19.0 0.0 copy-start.2
  19.0 0.5 collective-permute-start.6
  19.5 0.0 collective-permute-done.1.rest_2_
  19.5 0.0 copy-start.3
  19.5 1.5 %collective-permute-start.4 = (bf16[256,128]{1,0:T(8,128)(2,1)S(1)}, bf16[256,128]{1,0:T(8,128)(2,1)S(1)}, u32[]{:S(2)}, u32[]{:S(2)}) collective-permute-start(bf16[256,128]{1,0:T(8,128)(2,1)S(1)} %collective-permute-done.3.rest_4_), channel_id=1, source_target_pairs={{0,2},{2,0},{4,6},{6,4},{8,10},{10,8},{12,14},{14,12},{1,3},{3,1},... | collective-permute-start | bytes 196616 | tf_op jit(solution)/shard_map/ppermute | solution.py:341
  21.1 0.9 collective-permute-done.rest_1_
  21.9 0.0 copy-done.1
  21.9 0.0 copy-start.4
  21.9 2.0 %collective-permute-start.2 = (bf16[256,128]{1,0:T(8,128)(2,1)S(1)}, bf16[256,128]{1,0:T(8,128)(2,1)S(1)}, u32[]{:S(2)}, u32[]{:S(2)}) collective-permute-start(bf16[256,128]{1,0:T(8,128)(2,1)S(1)} %collective-permute-done.1.rest_2_), channel_id=1, source_target_pairs={{0,2},{2,0},{4,6},{6,4},{8,10},{10,8},{12,14},{14,12},{1,3},{3,1},... | collective-permute-start | bytes 196616 | tf_op jit(solution)/shard_map/ppermute | solution.py:341
  24.0 0.0 collective-permute-done.6.rest_7_
  24.0 0.0 copy-done.2
  24.0 0.0 copy-start.5
  24.0 0.0 collective-permute-done.4.rest_5_
  24.0 0.0 copy-done.3
  24.0 0.0 copy-start.6
  24.0 2.2 %collective-permute-done.2.rest_3_ = bf16[256,128]{1,0:T(8,128)(2,1)S(1)} collective-permute-done((bf16[256,128]{1,0:T(8,128)(2,1)S(1)}, bf16[256,128]{1,0:T(8,128)(2,1)S(1)}, u32[]{:S(2)}, u32[]{:S(2)}) %collective-permute-start.2) | collective-permute-done | bytes 65568 | tf_op jit(solution)/shard_map/ppermute | solution.py:341
  26.2 0.0 copy-done.4
  26.2 0.0 copy-start.7
  26.2 0.0 collective-permute-done.7.rest_9_
  26.2 0.0 copy-done.5
  26.2 0.0 collective-permute-done.8.rest_11_
  26.3 0.0 copy-done.6
  26.3 0.6 copy-done.7
  26.8 72.0 %flow.1 = f32[256,128]{1,0:T(8,128)} custom-call(s32[1]{0:T(128)} %bitcast.place_ref, s32[8]{0:T(128)} %frozen_ref.1, s32[3,8]{1,0:T(4,128)} %bitcast.6, bf16[128,384]{1,0:T(8,128)(2,1)} %get-tuple-element.7.gram_hbm, bf16[128,1536]{1,0:T(8,128)(2,1)} %embed_hbm.1, bf16[1536,256]{1,0:T(8,128)(2,1)} %head_hbm.1, bf16[256,128]{1,0:T(8,128)(2,1)} %copy-done, ...), custom_call_target="tpu_custom_call" | custom-call | tf_op jit(solution)/shard_map/flow/pallas_call | solution.py:309
Async XLA Ops:
  0.0 26.2 %collective-permute-start.8 = (bf16[768,1536]{1,0:T(8,128)(2,1)}, bf16[768,1536]{1,0:T(8,128)(2,1)}, u32[]{:S(2)}, u32[]{:S(2)}) collective-permute-start(bf16[768,1536]{1,0:T(8,128)(2,1)} %rest_10_.1), channel_id=1, source_target_pairs={{0,1},{1,0},{2,3},{3,2},{4,5},{5,4},{6,7},{7,6},{8,9},{9,8},{10,11... | collective-permute-start | bytes 7077896 | tf_op jit(solution)/shard_map/ppermute | solution.py:337
  6.6 19.6 %collective-permute-start.7 = (bf16[3,256,384]{2,1,0:T(8,128)(2,1)}, bf16[3,256,384]{2,1,0:T(8,128)(2,1)}, u32[]{:S(2)}, u32[]{:S(2)}) collective-permute-start(bf16[3,256,384]{2,1,0:T(8,128)(2,1)} %get-tuple-element.8.rest_8_), channel_id=1, source_target_pairs={{0,1},{1,0},{2,3},{3,2},{4,5},{5,4},{6,7},{7,6},{8,9},{9,8},{10,11... | collective-permute-start | bytes 1769480 | tf_op jit(solution)/shard_map/ppermute | solution.py:337
  10.0 7.5 %copy-start = (bf16[256,128]{1,0:T(8,128)(2,1)}, bf16[256,128]{1,0:T(8,128)(2,1)S(1)}, u32[]{:S(2)}) copy-start(bf16[256,128]{1,0:T(8,128)(2,1)S(1)} %fusion.rest_0_) | copy-start | bytes 196612
  10.0 7.5 %collective-permute-start.5 = (bf16[256,128]{1,0:T(8,128)(2,1)S(1)}, bf16[256,128]{1,0:T(8,128)(2,1)S(1)}, u32[]{:S(2)}, u32[]{:S(2)}) collective-permute-start(bf16[256,128]{1,0:T(8,128)(2,1)S(1)} %fusion.rest_0_), channel_id=1, source_target_pairs={{0,12},{2,14},{4,8},{6,10},{8,4},{10,6},{12,0},{14,2},{1,13},{3,15... | collective-permute-start | bytes 196616 | tf_op jit(solution)/shard_map/ppermute | solution.py:341
  11.6 7.4 %collective-permute-start.3 = (bf16[256,128]{1,0:T(8,128)(2,1)S(1)}, bf16[256,128]{1,0:T(8,128)(2,1)S(1)}, u32[]{:S(2)}, u32[]{:S(2)}) collective-permute-start(bf16[256,128]{1,0:T(8,128)(2,1)S(1)} %fusion.rest_0_), channel_id=1, source_target_pairs={{0,8},{2,10},{4,12},{6,14},{8,0},{10,2},{12,4},{14,6},{1,9},{3,11}... | collective-permute-start | bytes 196616 | tf_op jit(solution)/shard_map/ppermute | solution.py:341
  12.9 6.6 %collective-permute-start.1 = (bf16[256,128]{1,0:T(8,128)(2,1)S(1)}, bf16[256,128]{1,0:T(8,128)(2,1)S(1)}, u32[]{:S(2)}, u32[]{:S(2)}) collective-permute-start(bf16[256,128]{1,0:T(8,128)(2,1)S(1)} %fusion.rest_0_), channel_id=1, source_target_pairs={{0,4},{2,6},{4,0},{6,2},{8,12},{10,14},{12,8},{14,10},{1,5},{3,7},... | collective-permute-start | bytes 196616 | tf_op jit(solution)/shard_map/ppermute | solution.py:341
  17.5 4.4 %copy-start.1 = (bf16[256,128]{1,0:T(8,128)(2,1)}, bf16[256,128]{1,0:T(8,128)(2,1)S(1)}, u32[]{:S(2)}) copy-start(bf16[256,128]{1,0:T(8,128)(2,1)S(1)} %collective-permute-done.5.rest_6_) | copy-start | bytes 196612
  17.5 4.4 %collective-permute-start = (bf16[256,128]{1,0:T(8,128)(2,1)S(1)}, bf16[256,128]{1,0:T(8,128)(2,1)S(1)}, u32[]{:S(2)}, u32[]{:S(2)}) collective-permute-start(bf16[256,128]{1,0:T(8,128)(2,1)S(1)} %fusion.rest_0_), channel_id=1, source_target_pairs={{0,2},{2,0},{4,6},{6,4},{8,10},{10,8},{12,14},{14,12},{1,3},{3,1},... | collective-permute-start | bytes 196616 | tf_op jit(solution)/shard_map/ppermute | solution.py:341
  19.0 5.0 %copy-start.2 = (bf16[256,128]{1,0:T(8,128)(2,1)}, bf16[256,128]{1,0:T(8,128)(2,1)S(1)}, u32[]{:S(2)}) copy-start(bf16[256,128]{1,0:T(8,128)(2,1)S(1)} %collective-permute-done.3.rest_4_) | copy-start | bytes 196612
  19.0 5.0 %collective-permute-start.6 = (bf16[256,128]{1,0:T(8,128)(2,1)S(1)}, bf16[256,128]{1,0:T(8,128)(2,1)S(1)}, u32[]{:S(2)}, u32[]{:S(2)}) collective-permute-start(bf16[256,128]{1,0:T(8,128)(2,1)S(1)} %collective-permute-done.5.rest_6_), channel_id=1, source_target_pairs={{0,2},{2,0},{4,6},{6,4},{8,10},{10,8},{12,14},{14,12},{1,3},{3,1},... | collective-permute-start | bytes 196616 | tf_op jit(solution)/shard_map/ppermute | solution.py:341
  19.5 4.5 %copy-start.3 = (bf16[256,128]{1,0:T(8,128)(2,1)}, bf16[256,128]{1,0:T(8,128)(2,1)S(1)}, u32[]{:S(2)}) copy-start(bf16[256,128]{1,0:T(8,128)(2,1)S(1)} %collective-permute-done.1.rest_2_) | copy-start | bytes 196612
  19.5 4.5 %collective-permute-start.4 = (bf16[256,128]{1,0:T(8,128)(2,1)S(1)}, bf16[256,128]{1,0:T(8,128)(2,1)S(1)}, u32[]{:S(2)}, u32[]{:S(2)}) collective-permute-start(bf16[256,128]{1,0:T(8,128)(2,1)S(1)} %collective-permute-done.3.rest_4_), channel_id=1, source_target_pairs={{0,2},{2,0},{4,6},{6,4},{8,10},{10,8},{12,14},{14,12},{1,3},{3,1},... | collective-permute-start | bytes 196616 | tf_op jit(solution)/shard_map/ppermute | solution.py:341
  21.9 4.3 %copy-start.4 = (bf16[256,128]{1,0:T(8,128)(2,1)}, bf16[256,128]{1,0:T(8,128)(2,1)S(1)}, u32[]{:S(2)}) copy-start(bf16[256,128]{1,0:T(8,128)(2,1)S(1)} %collective-permute-done.rest_1_) | copy-start | bytes 196612
  21.9 4.3 %collective-permute-start.2 = (bf16[256,128]{1,0:T(8,128)(2,1)S(1)}, bf16[256,128]{1,0:T(8,128)(2,1)S(1)}, u32[]{:S(2)}, u32[]{:S(2)}) collective-permute-start(bf16[256,128]{1,0:T(8,128)(2,1)S(1)} %collective-permute-done.1.rest_2_), channel_id=1, source_target_pairs={{0,2},{2,0},{4,6},{6,4},{8,10},{10,8},{12,14},{14,12},{1,3},{3,1},... | collective-permute-start | bytes 196616 | tf_op jit(solution)/shard_map/ppermute | solution.py:341
  24.0 2.2 %copy-start.5 = (bf16[256,128]{1,0:T(8,128)(2,1)}, bf16[256,128]{1,0:T(8,128)(2,1)S(1)}, u32[]{:S(2)}) copy-start(bf16[256,128]{1,0:T(8,128)(2,1)S(1)} %collective-permute-done.6.rest_7_) | copy-start | bytes 196612
  24.0 2.3 %copy-start.6 = (bf16[256,128]{1,0:T(8,128)(2,1)}, bf16[256,128]{1,0:T(8,128)(2,1)S(1)}, u32[]{:S(2)}) copy-start(bf16[256,128]{1,0:T(8,128)(2,1)S(1)} %collective-permute-done.4.rest_5_) | copy-start | bytes 196612
  26.2 0.6 copy-start.7
where the time goes:
time: 99 us; the launch traced here: 98.8 us
  Pallas kernels  78.6 us (79%)
  starting transfers between devices  10.3 us (10%)
  waiting for transfers between devices  6.47 us (7%)
  local copies, waits for them, and re-layouts  1.84 us (2%)
    pallas_call x1, Pallas kernels, run_flow(): pl.pallas_call(functools.partial(flow_kernel, (frames, parts)), in_specs=...  72 us
    ppermute x7, starting transfers between devices, across(): lax.ppermute(value, axis, [(source, source ^ mask) for source in range(la...  9.71 us
    pallas_call x1, Pallas kernels, fold_weights(): pl.pallas_call(fold_kernel, in_specs=[vmem, pl.BlockSpec(memory_space=pl....  6.58 us
    ppermute x7, waiting for transfers between devices, across(): lax.ppermute(value, axis, [(source, source ^ mask) for source in range(la...  6.46 us
  transfers between devices with their start and end apart: 9, of which 3 were waited for; matrix products, arithmetic and copies ran while one was open for 2% of the time, Pallas kernels for 7%

commit v1 on v0

--- a/solution.py
+++ b/solution.py
@@ -24,13 +24,9 @@
     return out
 
 
-def fold_kernel(embed_ref, qkv_hbm, folded_ref, gram_ref, qkv, centred_ref, sems):
+def fold_kernel(embed_ref, qkv_ref, folded_ref, gram_ref, centred_ref):
     channels, width = embed_ref.shape
     pairs = folded_ref.shape[0]
-    loads = [pltpu.make_async_copy(qkv_hbm.at[index], qkv.at[index], sems.at[index]) for index in range(3)]
-    for load in loads:
-        load.start()
-
     rows = embed_ref[...].astype(F32)
     centred = rows - jnp.mean(rows, axis=1, keepdims=True)
     high, low = split_bf16(centred, 2)
@@ -49,8 +45,7 @@
     scale = math.log2(math.e) / math.sqrt(HD)
     maps = []
     for index in range(3):
-        loads[index].wait()
-        product = jnp.dot(centred_ref[...], qkv[index], preferred_element_type=F32)
+        product = jnp.dot(centred_ref[...], qkv_ref[index], preferred_element_type=F32)
         maps.append(product[:channels] + product[channels:])
         if index == 1:
             for head in range(2 * pairs):
@@ -82,18 +77,16 @@
     vmem = pl.BlockSpec(memory_space=pltpu.VMEM)
     return pl.pallas_call(
         fold_kernel,
-        in_specs=[vmem, pl.BlockSpec(memory_space=pl.ANY)],
+        in_specs=[vmem, vmem],
         out_specs=[vmem, vmem],
         out_shape=[
             jax.ShapeDtypeStruct((pairs, wide, channels + wide), BF16),
             jax.ShapeDtypeStruct((channels, 3 * channels), BF16),
         ],
         scratch_shapes=[
-            pltpu.VMEM((3, width, cols), BF16),
             pltpu.VMEM((2 * channels, width), BF16),
-            pltpu.SemaphoreType.DMA((3,)),
         ],
-        compiler_params=pltpu.CompilerParams(vmem_limit_bytes=67043328),
+        compiler_params=pltpu.CompilerParams(vmem_limit_bytes=24 * 1024 * 1024),
         cost_estimate=pl.CostEstimate(
             flops=4 * channels * width * 3 * cols, bytes_accessed=6 * width * cols, transcendentals=0
         ),
@@ -235,8 +228,8 @@
         residual = jnp.dot(attended[...], w_out[...], preferred_element_type=F32)
         centred = residual - jnp.mean(residual, axis=1, keepdims=True)
         spread_sq = jnp.mean(centred * centred, axis=1, keepdims=True)
-        head_in = (centred * lax.rsqrt(spread_sq + EPSILON)).astype(BF16)
-        return jnp.dot(head_in, w_head[...], preferred_element_type=F32)
+        predicted = jnp.dot(centred.astype(BF16), w_head[...], preferred_element_type=F32)
+        return predicted * lax.rsqrt(spread_sq + EPSILON)
 
     def moved(held, predicted):
         return held * jnp.exp(jnp.tanh(predicted[:, channels:])) + predicted[:, :channels]
@@ -294,6 +287,36 @@
         result_ref[...] = jnp.dot(flip(), raw[slot_of(target)], preferred_element_type=F32)
 
 
+def pick_kernel(place_ref, frozen_ref, latent_hbm, context_hbm, picked_ref, rows, sem):
+    held = frozen_ref[place_ref[0]] == 1
+
+    @pl.when(held)
+    def _():
+        pltpu.make_async_copy(context_hbm, rows, sem).start()
+
+    @pl.when(jnp.logical_not(held))
+    def _():
+        pltpu.make_async_copy(latent_hbm, rows, sem).start()
+
+    pltpu.make_async_copy(latent_hbm, rows, sem).wait()
+    picked_ref[...] = rows[...].astype(BF16)
+
+
+def pick_state(place, frozen, latent, context, cover):
+    smem = pl.BlockSpec(memory_space=pltpu.SMEM)
+    anywhere = pl.BlockSpec(memory_space=pl.ANY)
+    return pl.pallas_call(
+        pick_kernel,
+        in_specs=[smem, smem, anywhere, anywhere],
+        out_specs=pl.BlockSpec(memory_space=pltpu.VMEM),
+        out_shape=jax.ShapeDtypeStruct(latent.shape, BF16),
+        scratch_shapes=[pltpu.VMEM(latent.shape, F32), pltpu.SemaphoreType.DMA],
+        cost_estimate=pl.CostEstimate(flops=cover, bytes_accessed=4 * latent.size, transcendentals=0),
+        compiler_params=pltpu.CompilerParams(vmem_limit_bytes=4 * 1024 * 1024),
+        name="pick",
+    )(place, frozen, latent, context)
+
+
 def run_flow(place, frozen, read_list, blocks, gram, w_embed, w_head, folded, outs):
     tokens, channels = blocks[0].shape
     frames = len(blocks)
@@ -306,9 +329,10 @@
     smem = pl.BlockSpec(memory_space=pltpu.SMEM)
     anywhere = pl.BlockSpec(memory_space=pl.ANY)
     held = frames + slots
+    hbm = pl.BlockSpec(memory_space=pltpu.HBM)
     return pl.pallas_call(
         functools.partial(flow_kernel, (frames, parts)),
-        in_specs=[smem, smem, smem] + [anywhere] * (3 + frames + 2 * parts),
+        in_specs=[smem, smem, smem] + [anywhere] * 3 + [hbm] * frames + ([anywhere] + [hbm] * (parts - 1)) * 2,
         out_specs=vmem,
         out_shape=jax.ShapeDtypeStruct((tokens, channels), F32),
         scratch_shapes=[
@@ -327,7 +351,7 @@
             pltpu.SMEM((1,), jnp.int32),
             pltpu.SemaphoreType.DMA((frames + 3 + 2 * parts,)),
         ],
-        compiler_params=pltpu.CompilerParams(vmem_limit_bytes=67043328),
+        compiler_params=pltpu.CompilerParams(vmem_limit_bytes=40 * 1024 * 1024),
         name="flow",
     )(place, frozen, read_list, gram, w_embed, w_head, *blocks, *folded, *outs)
 
@@ -346,8 +370,9 @@
     seq_count = lax.axis_size("seq")
     clip_count = lax.axis_size("clip")
     layout = latent.shape
-    frozen_here = lax.dynamic_index_in_dim(frozen, position, 0, keepdims=False) == 1
-    held = jnp.where(frozen_here, context, latent).astype(BF16).reshape(layout[-2], layout[-1])
+    place = position.reshape(1).astype(jnp.int32)
+    rows = (layout[-2], layout[-1])
+    held = pick_state(place, frozen, latent.reshape(rows), context.reshape(rows), 6 * w_embed.shape[0] * w_qkv.size)
     blocks = [None] * seq_count
     blocks[0] = held
     for mask in [1] + list(range(2, seq_count, 2)):
@@ -358,7 +383,7 @@
     folded, gram = fold_weights(w_embed, w_qkv)
     folded = [folded] + [from_behind(folded, "clip", step) for step in range(1, clip_count)]
     result = run_flow(
-        position.reshape(1).astype(jnp.int32), frozen, read_list.T, blocks, gram, w_embed, w_head, folded, outs
+        place, frozen, read_list.T, blocks, gram, w_embed, w_head, folded, outs
     )
     return result.reshape(layout)
 

time: 99 us -> 98.7 us (level)
  local copies, waits for them, and re-layouts: 1.84 us -> 6.47 us
  Pallas kernels: 78.6 us -> 75.2 us
    unnamed x16 -> x22, local copies, waits for them, and re-layouts: 0.61 us -> 6.47 us
    pallas_call x1 -> x2, Pallas kernels: 6.58 us -> 3.38 us  [the longest x1 2.64 us: fold_weights(): pl.pallas_call(fold_kernel, in_specs=[vmem, vmem], out_specs=[vmem, vmem]...]
    dynamic_slice x1 -> x0, local copies, waits for them, and re-layouts: 1.24 us -> none  [per_device(): lax.dynamic_index_in_dim(frozen, position, 0, keepdims=False) == 1]
  transfers between devices with their start and end apart: 9 -> 9, of which waited for: 3 -> 3; matrix products, arithmetic and copies ran while one was open for 2% -> 0% of each run, Pallas kernels for 7% -> 3%
where the time goes in v1:
time: 98.7 us; the launch traced here: 98.5 us
  Pallas kernels  75.2 us (76%)
  starting transfers between devices  10.2 us (10%)
  waiting for transfers between devices  6.57 us (7%)
  local copies, waits for them, and re-layouts  6.47 us (7%)
    pallas_call x1, Pallas kernels, run_flow(): pl.pallas_call(functools.partial(flow_kernel, (frames, parts)), in_specs=...  71.9 us
    ppermute x7, starting transfers between devices, across(): lax.ppermute(value, axis, [(source, source ^ mask) for source in range(la...  9.66 us
    ppermute x7, waiting for transfers between devices, across(): lax.ppermute(value, axis, [(source, source ^ mask) for source in range(la...  6.56 us
    unnamed x22, local copies, waits for them, and re-layouts  6.47 us
    pallas_call x1, Pallas kernels, fold_weights(): pl.pallas_call(fold_kernel, in_specs=[vmem, vmem], out_specs=[vmem, vmem]...  2.64 us
  transfers between devices with their start and end apart: 9, of which 3 were waited for; matrix products, arithmetic and copies ran while one was open for 0% of the time, Pallas kernels for 3%

profile of v1, /device:TPU:10, one launch (start us, length us, event | category | flops | bytes accessed | tf_op | source)
XLA Modules:
  0.0 98.5 jit_solution(13589456393149799299)
XLA Ops:
  0.0 0.0 collective-permute-start.8
  0.0 0.0 copy-start
  0.0 3.0 %copy-done = bf16[3,1536,768]{2,1,0:T(8,128)(2,1)S(1)} copy-done((bf16[3,1536,768]{2,1,0:T(8,128)(2,1)S(1)}, bf16[3,1536,768]{2,1,0:T(8,128)(2,1)}, u32[]{:S(2)}) %copy-start) | copy-done | bytes 7077912
  3.0 0.0 copy-start.2
  3.0 1.0 %copy-done.2 = bf16[128,1536]{1,0:T(8,128)(2,1)S(1)} copy-done((bf16[128,1536]{1,0:T(8,128)(2,1)S(1)}, bf16[128,1536]{1,0:T(8,128)(2,1)}, u32[]{:S(2)}) %copy-start.2) | copy-done | bytes 393240
  4.0 0.0 copy-start.8
  4.0 2.6 %fold.1 = (bf16[3,256,384]{2,1,0:T(8,128)(2,1)S(1)}, bf16[128,384]{1,0:T(8,128)(2,1)S(1)}) custom-call(bf16[128,1536]{1,0:T(8,128)(2,1)S(1)} %copy-done.2, bf16[3,1536,768]{2,1,0:T(8,128)(2,1)S(1)} %copy-done), custom_call_target="tpu_custom_call" | custom-call | flops 1811939328 | bytes 7077888 | tf_op jit(solution)/shard_map/fold/pallas_call | solution.py:78
  6.7 0.0 copy-start.5
  6.7 0.6 copy-done.5
  7.3 0.5 collective-permute-start.7
  7.8 0.0 copy-done.8
  7.8 0.0 copy-start.9
  7.8 0.9 copy-done.9
  8.7 0.0 copy-start.10
  8.7 0.9 copy-done.10
  9.6 0.0 copy-start.1
  9.6 0.0 copy-start.3
  9.6 0.0 copy-start.4
  9.6 0.0 copy-start.6
  9.6 0.0 copy-start.7
  9.6 0.7 pick.1.rest_0_
  10.4 1.6 %collective-permute-start.5 = (bf16[256,128]{1,0:T(8,128)(2,1)S(1)}, bf16[256,128]{1,0:T(8,128)(2,1)S(1)}, u32[]{:S(2)}, u32[]{:S(2)}) collective-permute-start(bf16[256,128]{1,0:T(8,128)(2,1)S(1)} %pick.1.rest_0_), channel_id=1, source_target_pairs={{0,12},{2,14},{4,8},{6,10},{8,4},{10,6},{12,0},{14,2},{1,13},{3,15... | collective-permute-start | bytes 196616 | tf_op jit(solution)/shard_map/ppermute | solution.py:365
  12.0 1.2 %collective-permute-start.3 = (bf16[256,128]{1,0:T(8,128)(2,1)S(1)}, bf16[256,128]{1,0:T(8,128)(2,1)S(1)}, u32[]{:S(2)}, u32[]{:S(2)}) collective-permute-start(bf16[256,128]{1,0:T(8,128)(2,1)S(1)} %pick.1.rest_0_), channel_id=1, source_target_pairs={{0,8},{2,10},{4,12},{6,14},{8,0},{10,2},{12,4},{14,6},{1,9},{3,11}... | collective-permute-start | bytes 196616 | tf_op jit(solution)/shard_map/ppermute | solution.py:365
  13.3 1.2 %collective-permute-start.1 = (bf16[256,128]{1,0:T(8,128)(2,1)S(1)}, bf16[256,128]{1,0:T(8,128)(2,1)S(1)}, u32[]{:S(2)}, u32[]{:S(2)}) collective-permute-start(bf16[256,128]{1,0:T(8,128)(2,1)S(1)} %pick.1.rest_0_), channel_id=1, source_target_pairs={{0,4},{2,6},{4,0},{6,2},{8,12},{10,14},{12,8},{14,10},{1,5},{3,7},... | collective-permute-start | bytes 196616 | tf_op jit(solution)/shard_map/ppermute | solution.py:365
  14.5 3.3 %collective-permute-done.5.rest_6_ = bf16[256,128]{1,0:T(8,128)(2,1)S(1)} collective-permute-done((bf16[256,128]{1,0:T(8,128)(2,1)S(1)}, bf16[256,128]{1,0:T(8,128)(2,1)S(1)}, u32[]{:S(2)}, u32[]{:S(2)}) %collective-permute-start.5) | collective-permute-done | bytes 65568 | tf_op jit(solution)/shard_map/ppermute | solution.py:365
  17.9 1.5 %collective-permute-start = (bf16[256,128]{1,0:T(8,128)(2,1)S(1)}, bf16[256,128]{1,0:T(8,128)(2,1)S(1)}, u32[]{:S(2)}, u32[]{:S(2)}) collective-permute-start(bf16[256,128]{1,0:T(8,128)(2,1)S(1)} %pick.1.rest_0_), channel_id=1, source_target_pairs={{0,2},{2,0},{4,6},{6,4},{8,10},{10,8},{12,14},{14,12},{1,3},{3,1},... | collective-permute-start | bytes 196616 | tf_op jit(solution)/shard_map/ppermute | solution.py:365
  19.4 0.0 collective-permute-done.3.rest_4_
  19.4 0.5 collective-permute-start.6
  19.9 0.0 collective-permute-done.1.rest_2_
  19.9 1.5 %collective-permute-start.4 = (bf16[256,128]{1,0:T(8,128)(2,1)S(1)}, bf16[256,128]{1,0:T(8,128)(2,1)S(1)}, u32[]{:S(2)}, u32[]{:S(2)}) collective-permute-start(bf16[256,128]{1,0:T(8,128)(2,1)S(1)} %collective-permute-done.3.rest_4_), channel_id=1, source_target_pairs={{0,2},{2,0},{4,6},{6,4},{8,10},{10,8},{12,14},{14,12},{1,3},{3,1},... | collective-permute-start | bytes 196616 | tf_op jit(solution)/shard_map/ppermute | solution.py:365
  21.4 0.9 collective-permute-done.rest_1_
  22.4 2.0 %collective-permute-start.2 = (bf16[256,128]{1,0:T(8,128)(2,1)S(1)}, bf16[256,128]{1,0:T(8,128)(2,1)S(1)}, u32[]{:S(2)}, u32[]{:S(2)}) collective-permute-start(bf16[256,128]{1,0:T(8,128)(2,1)S(1)} %collective-permute-done.1.rest_2_), channel_id=1, source_target_pairs={{0,2},{2,0},{4,6},{6,4},{8,10},{10,8},{12,14},{14,12},{1,3},{3,1},... | collective-permute-start | bytes 196616 | tf_op jit(solution)/shard_map/ppermute | solution.py:365
  24.3 0.0 collective-permute-done.6.rest_7_
  24.3 0.0 collective-permute-done.4.rest_5_
  24.4 2.3 %collective-permute-done.2.rest_3_ = bf16[256,128]{1,0:T(8,128)(2,1)S(1)} collective-permute-done((bf16[256,128]{1,0:T(8,128)(2,1)S(1)}, bf16[256,128]{1,0:T(8,128)(2,1)S(1)}, u32[]{:S(2)}, u32[]{:S(2)}) %collective-permute-start.2) | collective-permute-done | bytes 65568 | tf_op jit(solution)/shard_map/ppermute | solution.py:365
  26.6 0.0 collective-permute-done.7.rest_9_
  26.6 0.0 collective-permute-done.8.rest_11_
  26.6 0.0 copy-done.1
  26.6 0.0 copy-done.3
  26.6 0.0 copy-done.4
  26.7 0.0 copy-done.6
  26.7 0.0 copy-done.7
  26.7 71.9 %flow.1 = f32[256,128]{1,0:T(8,128)} custom-call(s32[1]{0:T(128)} %bitcast.place_ref, s32[8]{0:T(128)S(1)} %copy-done.8, s32[3,8]{1,0:T(4,128)S(1)} %bitcast.5, bf16[128,384]{1,0:T(8,128)(2,1)S(1)} %copy-done.6, bf16[128,1536]{1,0:T(8,128)(2,1)S(1)} %copy-done.3, bf16[1536,256]{1,0:T(8,128)(2,1)S(1)} %copy-done.4, bf16[256,128]{1,0:T(8,128)(2,1)S(1)} %pick.1.rest_0_, ...), custom_call_target="tpu_custom_call" | custom-call | tf_op jit(solution)/shard_map/flow/pallas_call | solution.py:333
Async XLA Ops:
  0.0 26.6 %collective-permute-start.8 = (bf16[768,1536]{1,0:T(8,128)(2,1)}, bf16[768,1536]{1,0:T(8,128)(2,1)S(1)}, u32[]{:S(2)}, u32[]{:S(2)}) collective-permute-start(bf16[768,1536]{1,0:T(8,128)(2,1)} %rest_10_.1), channel_id=1, source_target_pairs={{0,1},{1,0},{2,3},{3,2},{4,5},{5,4},{6,7},{7,6},{8,9},{9,8},{10,11... | collective-permute-start | bytes 7077896 | tf_op jit(solution)/shard_map/ppermute | solution.py:361
  0.0 3.0 %copy-start = (bf16[3,1536,768]{2,1,0:T(8,128)(2,1)S(1)}, bf16[3,1536,768]{2,1,0:T(8,128)(2,1)}, u32[]{:S(2)}) copy-start(bf16[3,1536,768]{2,1,0:T(8,128)(2,1)} %qkv_ref.1) | copy-start | bytes 21233668
  3.0 1.0 %copy-start.2 = (bf16[128,1536]{1,0:T(8,128)(2,1)S(1)}, bf16[128,1536]{1,0:T(8,128)(2,1)}, u32[]{:S(2)}) copy-start(bf16[128,1536]{1,0:T(8,128)(2,1)} %embed_hbm.1) | copy-start | bytes 1179652
  4.0 3.8 %copy-start.8 = (s32[8]{0:T(128)S(1)}, s32[8]{0:T(128)}, u32[]{:S(2)}) copy-start(s32[8]{0:T(128)} %frozen_ref.3) | copy-start | bytes 100
  6.7 0.6 copy-start.5
  7.3 19.3 %collective-permute-start.7 = (bf16[3,256,384]{2,1,0:T(8,128)(2,1)S(1)}, bf16[3,256,384]{2,1,0:T(8,128)(2,1)S(1)}, u32[]{:S(2)}, u32[]{:S(2)}) collective-permute-start(bf16[3,256,384]{2,1,0:T(8,128)(2,1)S(1)} %get-tuple-element.8.rest_8_), channel_id=1, source_target_pairs={{0,1},{1,0},{2,3},{3,2},{4,5},{5,4},{6,7},{7,6},{8,9},{9,8},{10,11... | collective-permute-start | bytes 1769480 | tf_op jit(solution)/shard_map/ppermute | solution.py:361
  7.8 0.9 copy-start.9
  8.7 0.9 copy-start.10
  9.6 17.0 %copy-start.1 = (bf16[768,1536]{1,0:T(8,128)(2,1)S(1)}, bf16[768,1536]{1,0:T(8,128)(2,1)}, u32[]{:S(2)}) copy-start(bf16[768,1536]{1,0:T(8,128)(2,1)} %rest_10_.1) | copy-start | bytes 7077892
  9.6 17.0 %copy-start.3 = (bf16[128,1536]{1,0:T(8,128)(2,1)S(1)}, bf16[128,1536]{1,0:T(8,128)(2,1)}, u32[]{:S(2)}) copy-start(bf16[128,1536]{1,0:T(8,128)(2,1)} %embed_hbm.1) | copy-start | bytes 1179652
  9.6 17.0 %copy-start.4 = (bf16[1536,256]{1,0:T(8,128)(2,1)S(1)}, bf16[1536,256]{1,0:T(8,128)(2,1)}, u32[]{:S(2)}) copy-start(bf16[1536,256]{1,0:T(8,128)(2,1)} %head_hbm.1) | copy-start | bytes 2359300
  9.6 17.0 %copy-start.6 = (bf16[128,384]{1,0:T(8,128)(2,1)S(1)}, bf16[128,384]{1,0:T(8,128)(2,1)}, u32[]{:S(2)}) copy-start(bf16[128,384]{1,0:T(8,128)(2,1)} %copy-done.5) | copy-start | bytes 294916
  9.6 17.0 %copy-start.7 = (s32[8,3]{0,1:T(4,128)S(1)}, s32[8,3]{0,1:T(4,128)}, u32[]{:S(2)}) copy-start(s32[8,3]{0,1:T(4,128)} %param.11) | copy-start | bytes 292
  10.4 7.5 %collective-permute-start.5 = (bf16[256,128]{1,0:T(8,128)(2,1)S(1)}, bf16[256,128]{1,0:T(8,128)(2,1)S(1)}, u32[]{:S(2)}, u32[]{:S(2)}) collective-permute-start(bf16[256,128]{1,0:T(8,128)(2,1)S(1)} %pick.1.rest_0_), channel_id=1, source_target_pairs={{0,12},{2,14},{4,8},{6,10},{8,4},{10,6},{12,0},{14,2},{1,13},{3,15... | collective-permute-start | bytes 196616 | tf_op jit(solution)/shard_map/ppermute | solution.py:365
  12.0 7.3 %collective-permute-start.3 = (bf16[256,128]{1,0:T(8,128)(2,1)S(1)}, bf16[256,128]{1,0:T(8,128)(2,1)S(1)}, u32[]{:S(2)}, u32[]{:S(2)}) collective-permute-start(bf16[256,128]{1,0:T(8,128)(2,1)S(1)} %pick.1.rest_0_), channel_id=1, source_target_pairs={{0,8},{2,10},{4,12},{6,14},{8,0},{10,2},{12,4},{14,6},{1,9},{3,11}... | collective-permute-start | bytes 196616 | tf_op jit(solution)/shard_map/ppermute | solution.py:365
  13.3 6.6 %collective-permute-start.1 = (bf16[256,128]{1,0:T(8,128)(2,1)S(1)}, bf16[256,128]{1,0:T(8,128)(2,1)S(1)}, u32[]{:S(2)}, u32[]{:S(2)}) collective-permute-start(bf16[256,128]{1,0:T(8,128)(2,1)S(1)} %pick.1.rest_0_), channel_id=1, source_target_pairs={{0,4},{2,6},{4,0},{6,2},{8,12},{10,14},{12,8},{14,10},{1,5},{3,7},... | collective-permute-start | bytes 196616 | tf_op jit(solution)/shard_map/ppermute | solution.py:365
  17.9 4.5 %collective-permute-start = (bf16[256,128]{1,0:T(8,128)(2,1)S(1)}, bf16[256,128]{1,0:T(8,128)(2,1)S(1)}, u32[]{:S(2)}, u32[]{:S(2)}) collective-permute-start(bf16[256,128]{1,0:T(8,128)(2,1)S(1)} %pick.1.rest_0_), channel_id=1, source_target_pairs={{0,2},{2,0},{4,6},{6,4},{8,10},{10,8},{12,14},{14,12},{1,3},{3,1},... | collective-permute-start | bytes 196616 | tf_op jit(solution)/shard_map/ppermute | solution.py:365
  19.4 5.0 %collective-permute-start.6 = (bf16[256,128]{1,0:T(8,128)(2,1)S(1)}, bf16[256,128]{1,0:T(8,128)(2,1)S(1)}, u32[]{:S(2)}, u32[]{:S(2)}) collective-permute-start(bf16[256,128]{1,0:T(8,128)(2,1)S(1)} %collective-permute-done.5.rest_6_), channel_id=1, source_target_pairs={{0,2},{2,0},{4,6},{6,4},{8,10},{10,8},{12,14},{14,12},{1,3},{3,1},... | collective-permute-start | bytes 196616 | tf_op jit(solution)/shard_map/ppermute | solution.py:365
  19.9 4.5 %collective-permute-start.4 = (bf16[256,128]{1,0:T(8,128)(2,1)S(1)}, bf16[256,128]{1,0:T(8,128)(2,1)S(1)}, u32[]{:S(2)}, u32[]{:S(2)}) collective-permute-start(bf16[256,128]{1,0:T(8,128)(2,1)S(1)} %collective-permute-done.3.rest_4_), channel_id=1, source_target_pairs={{0,2},{2,0},{4,6},{6,4},{8,10},{10,8},{12,14},{14,12},{1,3},{3,1},... | collective-permute-start | bytes 196616 | tf_op jit(solution)/shard_map/ppermute | solution.py:365
  22.4 4.3 %collective-permute-start.2 = (bf16[256,128]{1,0:T(8,128)(2,1)S(1)}, bf16[256,128]{1,0:T(8,128)(2,1)S(1)}, u32[]{:S(2)}, u32[]{:S(2)}) collective-permute-start(bf16[256,128]{1,0:T(8,128)(2,1)S(1)} %collective-permute-done.1.rest_2_), channel_id=1, source_target_pairs={{0,2},{2,0},{4,6},{6,4},{8,10},{10,8},{12,14},{14,12},{1,3},{3,1},... | collective-permute-start | bytes 196616 | tf_op jit(solution)/shard_map/ppermute | solution.py:365

commit v2 on v1

--- a/solution.py
+++ b/solution.py
@@ -99,7 +99,7 @@
     block_hbm, rest = rest[:frames], rest[frames:]
     folded_hbm, out_hbm, rest = rest[:parts], rest[parts:2 * parts], rest[2 * parts:]
     (result_ref, raw, turned, straight, query, keys, values, mapped, attended,
-     folded, w_out, w_head, gram_ref, ready, sems) = rest
+     folded, w_out, w_head, gram_ref, predicted_ref, sems) = rest
     tokens, channels = raw.shape[1:]
     links = read_ref.shape[0]
     slots = links + 1
@@ -122,14 +122,6 @@
     late_loads.append(pltpu.make_async_copy(head_hbm, w_head, sems.at[frames + 2 * parts + 1]))
     for load in block_loads + folded_loads + late_loads:
         load.start()
-    ready[0] = 0
-
-    def await_late():
-        @pl.when(ready[0] == 0)
-        def _():
-            for load in late_loads:
-                load.wait()
-            ready[0] = 1
 
     def slot_of(frame):
         return jnp.bitwise_xor(place, frame)
@@ -146,7 +138,7 @@
 
     for load in block_loads:
         load.wait()
-    group = math.gcd(frames, 4)
+    group = math.gcd(frames, 8)
 
     def ingest_step(index, carry):
         for side in range(group):
@@ -155,7 +147,7 @@
         return carry
 
     lax.fori_loop(0, frames // group, ingest_step, 0)
-    for load in folded_loads:
+    for load in folded_loads + late_loads:
         load.wait()
 
     target = frames - 1 - place
@@ -192,40 +184,54 @@
 
     def attend():
         heads = 2 * folded.shape[0]
-        scores, contexts = scores_of(0, 0), []
+        queue, contexts = [scores_of(0, 0), scores_of(0, 1)], []
         fits = jnp.ones((1, tokens), F32)
         for head in range(heads):
-            following = scores_of((head + 1) // 2, (head + 1) % 2) if head + 1 < heads else None
-            context, mass = context_of(scores)
+            if head + 2 < heads:
+                queue.append(scores_of((head + 2) // 2, head % 2))
+            context, mass = context_of(queue.pop(0))
             fits = jnp.where(jnp.logical_and(mass > 2.0 ** -80, mass < 2.0 ** 110), fits, 0.0)
             contexts.append(context)
-            scores = following
             if head % 2:
                 pair = head // 2
                 attended[:, pair * 2 * HD:(pair + 1) * 2 * HD] = mix(pair, contexts)
                 contexts = []
 
-        @pl.when(jnp.min(fits) < 0.5)
-        def _():
-            def shifted_pair(pair, carry):
-                contexts = []
-                for side in range(2):
-                    scores = scores_of(pair, side)
-                    contexts.append(context_of(scores - jnp.max(scores, axis=0, keepdims=True))[0])
-                start = pl.multiple_of(pair * 2 * HD, 2 * HD)
-                attended[:, pl.ds(start, 2 * HD)] = mix(pair, contexts)
-                return carry
-
-            lax.fori_loop(0, folded.shape[0], shifted_pair, 0)
+        return jnp.min(fits)
+
+    def attend_shifted():
+        def shifted_pair(pair, carry):
+            contexts = []
+            for side in range(2):
+                scores = scores_of(pair, side)
+                contexts.append(context_of(scores - jnp.max(scores, axis=0, keepdims=True))[0])
+            start = pl.multiple_of(pair * 2 * HD, 2 * HD)
+            attended[:, pl.ds(start, 2 * HD)] = mix(pair, contexts)
+            return carry
+
+        lax.fori_loop(0, folded.shape[0], shifted_pair, 0)
 
     def evaluate():
         for pair in range(folded.shape[0]):
             mapped[pair] = jnp.dot(
                 folded[pair, :, :channels], query[...], preferred_element_type=F32
             ).astype(BF16)
-        attend()
-        await_late()
-        residual = jnp.dot(attended[...], w_out[...], preferred_element_type=F32)
+        fits = attend()
+        predicted_ref[...] = predict()
+
+        @pl.when(fits < 0.5)
+        def _():
+            attend_shifted()
+            predicted_ref[...] = predict()
+
+        return predicted_ref[...]
+
+    def predict():
+        halves = [slice(start, start + tokens // 2) for start in (0, tokens // 2)]
+        residuals = [jnp.dot(attended[rows], w_out[...], preferred_element_type=F32) for rows in halves]
+        return jnp.concatenate([finish(residual) for residual in residuals], axis=0)
+
+    def finish(residual):
         centred = residual - jnp.mean(residual, axis=1, keepdims=True)
         spread_sq = jnp.mean(centred * centred, axis=1, keepdims=True)
         predicted = jnp.dot(centred.astype(BF16), w_head[...], preferred_element_type=F32)
@@ -280,7 +286,6 @@
         return carry
 
     lax.fori_loop(0, slots + 1, round_step, 0)
-    await_late()
 
     @pl.when(jnp.logical_not(run_all))
     def _():
@@ -348,7 +353,7 @@
             pltpu.VMEM((hidden + channels, width), BF16),
             pltpu.VMEM(w_head.shape, BF16),
             pltpu.VMEM(gram.shape, BF16),
-            pltpu.SMEM((1,), jnp.int32),
+            pltpu.VMEM((tokens, w_head.shape[1]), F32),
             pltpu.SemaphoreType.DMA((frames + 3 + 2 * parts,)),
         ],
         compiler_params=pltpu.CompilerParams(vmem_limit_bytes=40 * 1024 * 1024),

time: 98.7 us -> 105 us (1.064)
  Pallas kernels: 75.2 us -> 81.3 us
    pallas_call x1, Pallas kernels: 71.9 us -> 77.8 us  [run_flow(): pl.pallas_call(functools.partial(flow_kernel, (frames, parts)), in_specs=...]
where the time goes in v2:
time: 105 us
  Pallas kernels  81.3 us (77%)
  starting transfers between devices  10.2 us (10%)
  waiting for transfers between devices  6.57 us (6%)
  local copies, waits for them, and re-layouts  6.47 us (6%)
    pallas_call x1, Pallas kernels, run_flow(): pl.pallas_call(functools.partial(flow_kernel, (frames, parts)), in_specs=...  77.8 us
    ppermute x7, starting transfers between devices, across(): lax.ppermute(value, axis, [(source, source ^ mask) for source in range(la...  9.66 us
    ppermute x7, waiting for transfers between devices, across(): lax.ppermute(value, axis, [(source, source ^ mask) for source in range(la...  6.56 us
    unnamed x22, local copies, waits for them, and re-layouts  6.47 us
    pallas_call x1, Pallas kernels, fold_weights(): pl.pallas_call(fold_kernel, in_specs=[vmem, vmem], out_specs=[vmem, vmem]...  2.64 us
  transfers between devices with their start and end apart: 9, of which 3 were waited for; matrix products, arithmetic and copies ran while one was open for 0% of the time, Pallas kernels for 3%

profile of v2, /device:TPU:10, one launch (start us, length us, event | category | flops | bytes accessed | tf_op | source)
XLA Modules:
  0.0 104.8 jit_solution(1416768767205490076)
XLA Ops:
  0.0 0.0 collective-permute-start.8
  0.0 0.0 copy-start
  0.0 3.0 %copy-done = bf16[3,1536,768]{2,1,0:T(8,128)(2,1)S(1)} copy-done((bf16[3,1536,768]{2,1,0:T(8,128)(2,1)S(1)}, bf16[3,1536,768]{2,1,0:T(8,128)(2,1)}, u32[]{:S(2)}) %copy-start) | copy-done | bytes 7077912
  3.0 0.0 copy-start.2
  3.0 1.0 copy-done.2
  4.0 0.0 copy-start.8
  4.0 2.6 %fold.1 = (bf16[3,256,384]{2,1,0:T(8,128)(2,1)S(1)}, bf16[128,384]{1,0:T(8,128)(2,1)S(1)}) custom-call(bf16[128,1536]{1,0:T(8,128)(2,1)S(1)} %copy-done.2, bf16[3,1536,768]{2,1,0:T(8,128)(2,1)S(1)} %copy-done), custom_call_target="tpu_custom_call" | custom-call | flops 1811939328 | bytes 7077888 | tf_op jit(solution)/shard_map/fold/pallas_call | solution.py:78
  6.7 0.0 copy-start.5
  6.7 0.6 copy-done.5
  7.3 0.5 collective-permute-start.7
  7.8 0.0 copy-done.8
  7.8 0.0 copy-start.9
  7.8 0.9 copy-done.9
  8.7 0.0 copy-start.10
  8.7 0.9 copy-done.10
  9.6 0.0 copy-start.1
  9.6 0.0 copy-start.3
  9.6 0.0 copy-start.4
  9.6 0.0 copy-start.6
  9.6 0.0 copy-start.7
  9.6 0.9 pick.1.rest_0_
  10.6 1.6 %collective-permute-start.5 = (bf16[256,128]{1,0:T(8,128)(2,1)S(1)}, bf16[256,128]{1,0:T(8,128)(2,1)S(1)}, u32[]{:S(2)}, u32[]{:S(2)}) collective-permute-start(bf16[256,128]{1,0:T(8,128)(2,1)S(1)} %pick.1.rest_0_), channel_id=1, source_target_pairs={{0,12},{2,14},{4,8},{6,10},{8,4},{10,6},{12,0},{14,2},{1,13},{3,15... | collective-permute-start | bytes 196616 | tf_op jit(solution)/shard_map/ppermute | solution.py:370
  12.2 1.2 %collective-permute-start.3 = (bf16[256,128]{1,0:T(8,128)(2,1)S(1)}, bf16[256,128]{1,0:T(8,128)(2,1)S(1)}, u32[]{:S(2)}, u32[]{:S(2)}) collective-permute-start(bf16[256,128]{1,0:T(8,128)(2,1)S(1)} %pick.1.rest_0_), channel_id=1, source_target_pairs={{0,8},{2,10},{4,12},{6,14},{8,0},{10,2},{12,4},{14,6},{1,9},{3,11}... | collective-permute-start | bytes 196616 | tf_op jit(solution)/shard_map/ppermute | solution.py:370
  13.5 1.2 %collective-permute-start.1 = (bf16[256,128]{1,0:T(8,128)(2,1)S(1)}, bf16[256,128]{1,0:T(8,128)(2,1)S(1)}, u32[]{:S(2)}, u32[]{:S(2)}) collective-permute-start(bf16[256,128]{1,0:T(8,128)(2,1)S(1)} %pick.1.rest_0_), channel_id=1, source_target_pairs={{0,4},{2,6},{4,0},{6,2},{8,12},{10,14},{12,8},{14,10},{1,5},{3,7},... | collective-permute-start | bytes 196616 | tf_op jit(solution)/shard_map/ppermute | solution.py:370
  14.7 3.3 %collective-permute-done.5.rest_6_ = bf16[256,128]{1,0:T(8,128)(2,1)S(1)} collective-permute-done((bf16[256,128]{1,0:T(8,128)(2,1)S(1)}, bf16[256,128]{1,0:T(8,128)(2,1)S(1)}, u32[]{:S(2)}, u32[]{:S(2)}) %collective-permute-start.5) | collective-permute-done | bytes 65568 | tf_op jit(solution)/shard_map/ppermute | solution.py:370
  18.0 1.5 %collective-permute-start = (bf16[256,128]{1,0:T(8,128)(2,1)S(1)}, bf16[256,128]{1,0:T(8,128)(2,1)S(1)}, u32[]{:S(2)}, u32[]{:S(2)}) collective-permute-start(bf16[256,128]{1,0:T(8,128)(2,1)S(1)} %pick.1.rest_0_), channel_id=1, source_target_pairs={{0,2},{2,0},{4,6},{6,4},{8,10},{10,8},{12,14},{14,12},{1,3},{3,1},... | collective-permute-start | bytes 196616 | tf_op jit(solution)/shard_map/ppermute | solution.py:370
  19.6 0.0 collective-permute-done.3.rest_4_
  19.6 0.5 collective-permute-start.6
  20.1 0.0 collective-permute-done.1.rest_2_
  20.1 1.5 %collective-permute-start.4 = (bf16[256,128]{1,0:T(8,128)(2,1)S(1)}, bf16[256,128]{1,0:T(8,128)(2,1)S(1)}, u32[]{:S(2)}, u32[]{:S(2)}) collective-permute-start(bf16[256,128]{1,0:T(8,128)(2,1)S(1)} %collective-permute-done.3.rest_4_), channel_id=1, source_target_pairs={{0,2},{2,0},{4,6},{6,4},{8,10},{10,8},{12,14},{14,12},{1,3},{3,1},... | collective-permute-start | bytes 196616 | tf_op jit(solution)/shard_map/ppermute | solution.py:370
  21.6 0.9 collective-permute-done.rest_1_
  22.5 2.0 %collective-permute-start.2 = (bf16[256,128]{1,0:T(8,128)(2,1)S(1)}, bf16[256,128]{1,0:T(8,128)(2,1)S(1)}, u32[]{:S(2)}, u32[]{:S(2)}) collective-permute-start(bf16[256,128]{1,0:T(8,128)(2,1)S(1)} %collective-permute-done.1.rest_2_), channel_id=1, source_target_pairs={{0,2},{2,0},{4,6},{6,4},{8,10},{10,8},{12,14},{14,12},{1,3},{3,1},... | collective-permute-start | bytes 196616 | tf_op jit(solution)/shard_map/ppermute | solution.py:370
  24.5 0.0 collective-permute-done.6.rest_7_
  24.5 0.0 collective-permute-done.4.rest_5_
  24.5 2.3 %collective-permute-done.2.rest_3_ = bf16[256,128]{1,0:T(8,128)(2,1)S(1)} collective-permute-done((bf16[256,128]{1,0:T(8,128)(2,1)S(1)}, bf16[256,128]{1,0:T(8,128)(2,1)S(1)}, u32[]{:S(2)}, u32[]{:S(2)}) %collective-permute-start.2) | collective-permute-done | bytes 65568 | tf_op jit(solution)/shard_map/ppermute | solution.py:370
  26.8 0.0 collective-permute-done.7.rest_9_
  26.8 0.0 collective-permute-done.8.rest_11_
  26.8 0.0 copy-done.1
  26.8 0.0 copy-done.3
  26.8 0.0 copy-done.4
  26.8 0.0 copy-done.6
  26.8 0.0 copy-done.7
  26.9 77.8 %flow.1 = f32[256,128]{1,0:T(8,128)} custom-call(s32[1]{0:T(128)} %bitcast.place_ref, s32[8]{0:T(128)S(1)} %copy-done.8, s32[3,8]{1,0:T(4,128)S(1)} %bitcast.5, bf16[128,384]{1,0:T(8,128)(2,1)S(1)} %copy-done.6, bf16[128,1536]{1,0:T(8,128)(2,1)S(1)} %copy-done.3, bf16[1536,256]{1,0:T(8,128)(2,1)S(1)} %copy-done.4, bf16[256,128]{1,0:T(8,128)(2,1)S(1)} %pick.1.rest_0_, ...), custom_call_target="tpu_custom_call" | custom-call | tf_op jit(solution)/shard_map/flow/pallas_call | solution.py:338
Async XLA Ops:
  0.0 26.8 %collective-permute-start.8 = (bf16[768,1536]{1,0:T(8,128)(2,1)}, bf16[768,1536]{1,0:T(8,128)(2,1)S(1)}, u32[]{:S(2)}, u32[]{:S(2)}) collective-permute-start(bf16[768,1536]{1,0:T(8,128)(2,1)} %rest_10_.1), channel_id=1, source_target_pairs={{0,1},{1,0},{2,3},{3,2},{4,5},{5,4},{6,7},{7,6},{8,9},{9,8},{10,11... | collective-permute-start | bytes 7077896 | tf_op jit(solution)/shard_map/ppermute | solution.py:366
  0.0 3.0 %copy-start = (bf16[3,1536,768]{2,1,0:T(8,128)(2,1)S(1)}, bf16[3,1536,768]{2,1,0:T(8,128)(2,1)}, u32[]{:S(2)}) copy-start(bf16[3,1536,768]{2,1,0:T(8,128)(2,1)} %qkv_ref.1) | copy-start | bytes 21233668
  3.0 1.0 copy-start.2
  4.0 3.8 %copy-start.8 = (s32[8]{0:T(128)S(1)}, s32[8]{0:T(128)}, u32[]{:S(2)}) copy-start(s32[8]{0:T(128)} %frozen_ref.3) | copy-start | bytes 100
  6.7 0.6 copy-start.5
  7.3 19.5 %collective-permute-start.7 = (bf16[3,256,384]{2,1,0:T(8,128)(2,1)S(1)}, bf16[3,256,384]{2,1,0:T(8,128)(2,1)S(1)}, u32[]{:S(2)}, u32[]{:S(2)}) collective-permute-start(bf16[3,256,384]{2,1,0:T(8,128)(2,1)S(1)} %get-tuple-element.8.rest_8_), channel_id=1, source_target_pairs={{0,1},{1,0},{2,3},{3,2},{4,5},{5,4},{6,7},{7,6},{8,9},{9,8},{10,11... | collective-permute-start | bytes 1769480 | tf_op jit(solution)/shard_map/ppermute | solution.py:366
  7.8 0.9 copy-start.9
  8.7 0.9 copy-start.10
  9.6 17.2 %copy-start.1 = (bf16[768,1536]{1,0:T(8,128)(2,1)S(1)}, bf16[768,1536]{1,0:T(8,128)(2,1)}, u32[]{:S(2)}) copy-start(bf16[768,1536]{1,0:T(8,128)(2,1)} %rest_10_.1) | copy-start | bytes 7077892
  9.6 17.2 %copy-start.3 = (bf16[128,1536]{1,0:T(8,128)(2,1)S(1)}, bf16[128,1536]{1,0:T(8,128)(2,1)}, u32[]{:S(2)}) copy-start(bf16[128,1536]{1,0:T(8,128)(2,1)} %embed_hbm.1) | copy-start | bytes 1179652
  9.6 17.2 %copy-start.4 = (bf16[1536,256]{1,0:T(8,128)(2,1)S(1)}, bf16[1536,256]{1,0:T(8,128)(2,1)}, u32[]{:S(2)}) copy-start(bf16[1536,256]{1,0:T(8,128)(2,1)} %head_hbm.1) | copy-start | bytes 2359300
  9.6 17.2 %copy-start.6 = (bf16[128,384]{1,0:T(8,128)(2,1)S(1)}, bf16[128,384]{1,0:T(8,128)(2,1)}, u32[]{:S(2)}) copy-start(bf16[128,384]{1,0:T(8,128)(2,1)} %copy-done.5) | copy-start | bytes 294916
  9.6 17.2 %copy-start.7 = (s32[8,3]{0,1:T(4,128)S(1)}, s32[8,3]{0,1:T(4,128)}, u32[]{:S(2)}) copy-start(s32[8,3]{0,1:T(4,128)} %param.11) | copy-start | bytes 292
  10.6 7.5 %collective-permute-start.5 = (bf16[256,128]{1,0:T(8,128)(2,1)S(1)}, bf16[256,128]{1,0:T(8,128)(2,1)S(1)}, u32[]{:S(2)}, u32[]{:S(2)}) collective-permute-start(bf16[256,128]{1,0:T(8,128)(2,1)S(1)} %pick.1.rest_0_), channel_id=1, source_target_pairs={{0,12},{2,14},{4,8},{6,10},{8,4},{10,6},{12,0},{14,2},{1,13},{3,15... | collective-permute-start | bytes 196616 | tf_op jit(solution)/shard_map/ppermute | solution.py:370
  12.2 7.3 %collective-permute-start.3 = (bf16[256,128]{1,0:T(8,128)(2,1)S(1)}, bf16[256,128]{1,0:T(8,128)(2,1)S(1)}, u32[]{:S(2)}, u32[]{:S(2)}) collective-permute-start(bf16[256,128]{1,0:T(8,128)(2,1)S(1)} %pick.1.rest_0_), channel_id=1, source_target_pairs={{0,8},{2,10},{4,12},{6,14},{8,0},{10,2},{12,4},{14,6},{1,9},{3,11}... | collective-permute-start | bytes 196616 | tf_op jit(solution)/shard_map/ppermute | solution.py:370
  13.5 6.6 %collective-permute-start.1 = (bf16[256,128]{1,0:T(8,128)(2,1)S(1)}, bf16[256,128]{1,0:T(8,128)(2,1)S(1)}, u32[]{:S(2)}, u32[]{:S(2)}) collective-permute-start(bf16[256,128]{1,0:T(8,128)(2,1)S(1)} %pick.1.rest_0_), channel_id=1, source_target_pairs={{0,4},{2,6},{4,0},{6,2},{8,12},{10,14},{12,8},{14,10},{1,5},{3,7},... | collective-permute-start | bytes 196616 | tf_op jit(solution)/shard_map/ppermute | solution.py:370
  18.0 4.5 %collective-permute-start = (bf16[256,128]{1,0:T(8,128)(2,1)S(1)}, bf16[256,128]{1,0:T(8,128)(2,1)S(1)}, u32[]{:S(2)}, u32[]{:S(2)}) collective-permute-start(bf16[256,128]{1,0:T(8,128)(2,1)S(1)} %pick.1.rest_0_), channel_id=1, source_target_pairs={{0,2},{2,0},{4,6},{6,4},{8,10},{10,8},{12,14},{14,12},{1,3},{3,1},... | collective-permute-start | bytes 196616 | tf_op jit(solution)/shard_map/ppermute | solution.py:370
  19.6 5.0 %collective-permute-start.6 = (bf16[256,128]{1,0:T(8,128)(2,1)S(1)}, bf16[256,128]{1,0:T(8,128)(2,1)S(1)}, u32[]{:S(2)}, u32[]{:S(2)}) collective-permute-start(bf16[256,128]{1,0:T(8,128)(2,1)S(1)} %collective-permute-done.5.rest_6_), channel_id=1, source_target_pairs={{0,2},{2,0},{4,6},{6,4},{8,10},{10,8},{12,14},{14,12},{1,3},{3,1},... | collective-permute-start | bytes 196616 | tf_op jit(solution)/shard_map/ppermute | solution.py:370
  20.1 4.5 %collective-permute-start.4 = (bf16[256,128]{1,0:T(8,128)(2,1)S(1)}, bf16[256,128]{1,0:T(8,128)(2,1)S(1)}, u32[]{:S(2)}, u32[]{:S(2)}) collective-permute-start(bf16[256,128]{1,0:T(8,128)(2,1)S(1)} %collective-permute-done.3.rest_4_), channel_id=1, source_target_pairs={{0,2},{2,0},{4,6},{6,4},{8,10},{10,8},{12,14},{14,12},{1,3},{3,1},... | collective-permute-start | bytes 196616 | tf_op jit(solution)/shard_map/ppermute | solution.py:370
  22.5 4.3 %collective-permute-start.2 = (bf16[256,128]{1,0:T(8,128)(2,1)S(1)}, bf16[256,128]{1,0:T(8,128)(2,1)S(1)}, u32[]{:S(2)}, u32[]{:S(2)}) collective-permute-start(bf16[256,128]{1,0:T(8,128)(2,1)S(1)} %collective-permute-done.1.rest_2_), channel_id=1, source_target_pairs={{0,2},{2,0},{4,6},{6,4},{8,10},{10,8},{12,14},{14,12},{1,3},{3,1},... | collective-permute-start | bytes 196616 | tf_op jit(solution)/shard_map/ppermute | solution.py:370

commit v3 on v2

--- a/solution.py
+++ b/solution.py
@@ -292,34 +292,42 @@
         result_ref[...] = jnp.dot(flip(), raw[slot_of(target)], preferred_element_type=F32)
 
 
-def pick_kernel(place_ref, frozen_ref, latent_hbm, context_hbm, picked_ref, rows, sem):
-    held = frozen_ref[place_ref[0]] == 1
-
-    @pl.when(held)
-    def _():
-        pltpu.make_async_copy(context_hbm, rows, sem).start()
-
-    @pl.when(jnp.logical_not(held))
-    def _():
-        pltpu.make_async_copy(latent_hbm, rows, sem).start()
-
-    pltpu.make_async_copy(latent_hbm, rows, sem).wait()
-    picked_ref[...] = rows[...].astype(BF16)
+def pick_kernel(place_ref, frozen_hbm, latent_hbm, context_hbm, picked_ref, rows, flags, sem, flag_sem):
+    flag_load = pltpu.make_async_copy(frozen_hbm, flags, flag_sem)
+    row_loads = [
+        pltpu.make_async_copy(latent_hbm, rows.at[0], sem.at[0]),
+        pltpu.make_async_copy(context_hbm, rows.at[1], sem.at[1]),
+    ]
+    for load in [flag_load] + row_loads:
+        load.start()
+    for load in [flag_load] + row_loads:
+        load.wait()
+    picked_ref[...] = rows[jnp.where(flags[place_ref[0]] == 1, 1, 0)].astype(BF16)
 
 
 def pick_state(place, frozen, latent, context, cover):
     smem = pl.BlockSpec(memory_space=pltpu.SMEM)
-    anywhere = pl.BlockSpec(memory_space=pl.ANY)
+    hbm = pl.BlockSpec(memory_space=pltpu.HBM)
     return pl.pallas_call(
         pick_kernel,
-        in_specs=[smem, smem, anywhere, anywhere],
+        in_specs=[smem, hbm, hbm, hbm],
         out_specs=pl.BlockSpec(memory_space=pltpu.VMEM),
         out_shape=jax.ShapeDtypeStruct(latent.shape, BF16),
-        scratch_shapes=[pltpu.VMEM(latent.shape, F32), pltpu.SemaphoreType.DMA],
+        scratch_shapes=[
+            pltpu.VMEM((2,) + latent.shape, F32),
+            pltpu.SMEM(frozen.shape, jnp.int32),
+            pltpu.SemaphoreType.DMA((2,)),
+            pltpu.SemaphoreType.DMA,
+        ],
         cost_estimate=pl.CostEstimate(flops=cover, bytes_accessed=4 * latent.size, transcendentals=0),
         compiler_params=pltpu.CompilerParams(vmem_limit_bytes=4 * 1024 * 1024),
         name="pick",
-    )(place, frozen, latent, context)
+    )(
+        place,
+        pltpu.with_memory_space_constraint(frozen, pltpu.HBM),
+        pltpu.with_memory_space_constraint(latent, pltpu.HBM),
+        pltpu.with_memory_space_constraint(context, pltpu.HBM),
+    )
 
 
 def run_flow(place, frozen, read_list, blocks, gram, w_embed, w_head, folded, outs):

time: 105 us -> 104 us (level)
  local copies, waits for them, and re-layouts: 6.47 us -> 4.67 us
    unnamed x22 -> x18, local copies, waits for them, and re-layouts: 6.47 us -> 4.67 us
  transfers between devices with their start and end apart: 9 -> 9, of which waited for: 3 -> 3; matrix products, arithmetic and copies ran while one was open for 0% -> 0% of each run, Pallas kernels for 3% -> 4%
where the time goes in v3:
time: 104 us; the launch traced here: 103 us
  Pallas kernels  81.8 us (79%)
  starting transfers between devices  10.2 us (10%)
  waiting for transfers between devices  6.59 us (6%)
  local copies, waits for them, and re-layouts  4.67 us (4%)
    pallas_call x1, Pallas kernels, run_flow(): pl.pallas_call(functools.partial(flow_kernel, (frames, parts)), in_specs=...  78 us
    ppermute x7, starting transfers between devices, across(): lax.ppermute(value, axis, [(source, source ^ mask) for source in range(la...  9.65 us
    ppermute x7, waiting for transfers between devices, across(): lax.ppermute(value, axis, [(source, source ^ mask) for source in range(la...  6.59 us
    unnamed x18, local copies, waits for them, and re-layouts  4.67 us
    pallas_call x1, Pallas kernels, fold_weights(): pl.pallas_call(fold_kernel, in_specs=[vmem, vmem], out_specs=[vmem, vmem]...  2.64 us
  transfers between devices with their start and end apart: 9, of which 3 were waited for; matrix products, arithmetic and copies ran while one was open for 0% of the time, Pallas kernels for 4%

profile of v3, /device:TPU:10, one launch (start us, length us, event | category | flops | bytes accessed | tf_op | source)
XLA Modules:
  0.0 103.4 jit_solution(4946391762794645889)
XLA Ops:
  0.0 0.0 collective-permute-start.8
  0.0 0.0 copy-start
  0.0 3.0 %copy-done = bf16[3,1536,768]{2,1,0:T(8,128)(2,1)S(1)} copy-done((bf16[3,1536,768]{2,1,0:T(8,128)(2,1)S(1)}, bf16[3,1536,768]{2,1,0:T(8,128)(2,1)}, u32[]{:S(2)}) %copy-start) | copy-done | bytes 7077912
  3.0 0.0 copy-start.2
  3.0 1.0 copy-done.2
  4.0 2.6 %fold.1 = (bf16[3,256,384]{2,1,0:T(8,128)(2,1)S(1)}, bf16[128,384]{1,0:T(8,128)(2,1)S(1)}) custom-call(bf16[128,1536]{1,0:T(8,128)(2,1)S(1)} %copy-done.2, bf16[3,1536,768]{2,1,0:T(8,128)(2,1)S(1)} %copy-done), custom_call_target="tpu_custom_call" | custom-call | flops 1811939328 | bytes 7077888 | tf_op jit(solution)/shard_map/fold/pallas_call | solution.py:78
  6.7 0.0 copy-start.5
  6.7 0.6 copy-done.5
  7.3 0.5 collective-permute-start.7
  7.8 0.0 copy-start.1
  7.8 0.0 copy-start.3
  7.8 0.0 copy-start.4
  7.8 0.0 copy-start.6
  7.8 0.0 copy-start.7
  7.8 0.0 copy-start.8
  7.8 1.2 %pick.1.rest_0_ = bf16[256,128]{1,0:T(8,128)(2,1)S(1)} custom-call(s32[1]{0:T(128)} %bitcast.place_ref, s32[8]{0:T(128)} %frozen_ref.1, f32[256,128]{1,0:T(8,128)} %bitcast.6, f32[256,128]{1,0:T(8,128)} %bitcast.7), custom_call_target="tpu_custom_call" | custom-call | flops 2717908992 | bytes 131072 | tf_op jit(solution)/shard_map/pick/pallas_call | solution.py:311
  9.0 1.6 %collective-permute-start.5 = (bf16[256,128]{1,0:T(8,128)(2,1)S(1)}, bf16[256,128]{1,0:T(8,128)(2,1)S(1)}, u32[]{:S(2)}, u32[]{:S(2)}) collective-permute-start(bf16[256,128]{1,0:T(8,128)(2,1)S(1)} %pick.1.rest_0_), channel_id=1, source_target_pairs={{0,12},{2,14},{4,8},{6,10},{8,4},{10,6},{12,0},{14,2},{1,13},{3,15... | collective-permute-start | bytes 196616 | tf_op jit(solution)/shard_map/ppermute | solution.py:378
  10.6 1.2 %collective-permute-start.3 = (bf16[256,128]{1,0:T(8,128)(2,1)S(1)}, bf16[256,128]{1,0:T(8,128)(2,1)S(1)}, u32[]{:S(2)}, u32[]{:S(2)}) collective-permute-start(bf16[256,128]{1,0:T(8,128)(2,1)S(1)} %pick.1.rest_0_), channel_id=1, source_target_pairs={{0,8},{2,10},{4,12},{6,14},{8,0},{10,2},{12,4},{14,6},{1,9},{3,11}... | collective-permute-start | bytes 196616 | tf_op jit(solution)/shard_map/ppermute | solution.py:378
  11.9 1.2 %collective-permute-start.1 = (bf16[256,128]{1,0:T(8,128)(2,1)S(1)}, bf16[256,128]{1,0:T(8,128)(2,1)S(1)}, u32[]{:S(2)}, u32[]{:S(2)}) collective-permute-start(bf16[256,128]{1,0:T(8,128)(2,1)S(1)} %pick.1.rest_0_), channel_id=1, source_target_pairs={{0,4},{2,6},{4,0},{6,2},{8,12},{10,14},{12,8},{14,10},{1,5},{3,7},... | collective-permute-start | bytes 196616 | tf_op jit(solution)/shard_map/ppermute | solution.py:378
  13.1 3.4 %collective-permute-done.5.rest_6_ = bf16[256,128]{1,0:T(8,128)(2,1)S(1)} collective-permute-done((bf16[256,128]{1,0:T(8,128)(2,1)S(1)}, bf16[256,128]{1,0:T(8,128)(2,1)S(1)}, u32[]{:S(2)}, u32[]{:S(2)}) %collective-permute-start.5) | collective-permute-done | bytes 65568 | tf_op jit(solution)/shard_map/ppermute | solution.py:378
  16.5 1.5 %collective-permute-start = (bf16[256,128]{1,0:T(8,128)(2,1)S(1)}, bf16[256,128]{1,0:T(8,128)(2,1)S(1)}, u32[]{:S(2)}, u32[]{:S(2)}) collective-permute-start(bf16[256,128]{1,0:T(8,128)(2,1)S(1)} %pick.1.rest_0_), channel_id=1, source_target_pairs={{0,2},{2,0},{4,6},{6,4},{8,10},{10,8},{12,14},{14,12},{1,3},{3,1},... | collective-permute-start | bytes 196616 | tf_op jit(solution)/shard_map/ppermute | solution.py:378
  18.0 0.0 collective-permute-done.3.rest_4_
  18.0 0.5 collective-permute-start.6
  18.5 0.0 collective-permute-done.1.rest_2_
  18.5 1.5 %collective-permute-start.4 = (bf16[256,128]{1,0:T(8,128)(2,1)S(1)}, bf16[256,128]{1,0:T(8,128)(2,1)S(1)}, u32[]{:S(2)}, u32[]{:S(2)}) collective-permute-start(bf16[256,128]{1,0:T(8,128)(2,1)S(1)} %collective-permute-done.3.rest_4_), channel_id=1, source_target_pairs={{0,2},{2,0},{4,6},{6,4},{8,10},{10,8},{12,14},{14,12},{1,3},{3,1},... | collective-permute-start | bytes 196616 | tf_op jit(solution)/shard_map/ppermute | solution.py:378
  20.0 0.9 collective-permute-done.rest_1_
  21.0 2.0 %collective-permute-start.2 = (bf16[256,128]{1,0:T(8,128)(2,1)S(1)}, bf16[256,128]{1,0:T(8,128)(2,1)S(1)}, u32[]{:S(2)}, u32[]{:S(2)}) collective-permute-start(bf16[256,128]{1,0:T(8,128)(2,1)S(1)} %collective-permute-done.1.rest_2_), channel_id=1, source_target_pairs={{0,2},{2,0},{4,6},{6,4},{8,10},{10,8},{12,14},{14,12},{1,3},{3,1},... | collective-permute-start | bytes 196616 | tf_op jit(solution)/shard_map/ppermute | solution.py:378
  23.0 0.0 collective-permute-done.6.rest_7_
  23.0 0.0 collective-permute-done.4.rest_5_
  23.0 2.3 %collective-permute-done.2.rest_3_ = bf16[256,128]{1,0:T(8,128)(2,1)S(1)} collective-permute-done((bf16[256,128]{1,0:T(8,128)(2,1)S(1)}, bf16[256,128]{1,0:T(8,128)(2,1)S(1)}, u32[]{:S(2)}, u32[]{:S(2)}) %collective-permute-start.2) | collective-permute-done | bytes 65568 | tf_op jit(solution)/shard_map/ppermute | solution.py:378
  25.2 0.0 collective-permute-done.7.rest_9_
  25.3 0.0 collective-permute-done.8.rest_11_
  25.3 0.0 copy-done.1
  25.3 0.0 copy-done.3
  25.3 0.0 copy-done.4
  25.3 0.0 copy-done.6
  25.3 0.0 copy-done.7
  25.3 0.0 copy-done.8
  25.3 78.0 %flow.1 = f32[256,128]{1,0:T(8,128)} custom-call(s32[1]{0:T(128)} %bitcast.place_ref, s32[8]{0:T(128)S(1)} %copy-done.8, s32[3,8]{1,0:T(4,128)S(1)} %bitcast.5, bf16[128,384]{1,0:T(8,128)(2,1)S(1)} %copy-done.6, bf16[128,1536]{1,0:T(8,128)(2,1)S(1)} %copy-done.3, bf16[1536,256]{1,0:T(8,128)(2,1)S(1)} %copy-done.4, bf16[256,128]{1,0:T(8,128)(2,1)S(1)} %pick.1.rest_0_, ...), custom_call_target="tpu_custom_call" | custom-call | tf_op jit(solution)/shard_map/flow/pallas_call | solution.py:346
Async XLA Ops:
  0.0 25.3 %collective-permute-start.8 = (bf16[768,1536]{1,0:T(8,128)(2,1)}, bf16[768,1536]{1,0:T(8,128)(2,1)S(1)}, u32[]{:S(2)}, u32[]{:S(2)}) collective-permute-start(bf16[768,1536]{1,0:T(8,128)(2,1)} %rest_10_.1), channel_id=1, source_target_pairs={{0,1},{1,0},{2,3},{3,2},{4,5},{5,4},{6,7},{7,6},{8,9},{9,8},{10,11... | collective-permute-start | bytes 7077896 | tf_op jit(solution)/shard_map/ppermute | solution.py:374
  0.0 3.0 %copy-start = (bf16[3,1536,768]{2,1,0:T(8,128)(2,1)S(1)}, bf16[3,1536,768]{2,1,0:T(8,128)(2,1)}, u32[]{:S(2)}) copy-start(bf16[3,1536,768]{2,1,0:T(8,128)(2,1)} %qkv_ref.1) | copy-start | bytes 21233668
  3.0 1.0 copy-start.2
  6.7 0.6 copy-start.5
  7.3 18.0 %collective-permute-start.7 = (bf16[3,256,384]{2,1,0:T(8,128)(2,1)S(1)}, bf16[3,256,384]{2,1,0:T(8,128)(2,1)S(1)}, u32[]{:S(2)}, u32[]{:S(2)}) collective-permute-start(bf16[3,256,384]{2,1,0:T(8,128)(2,1)S(1)} %get-tuple-element.8.rest_8_), channel_id=1, source_target_pairs={{0,1},{1,0},{2,3},{3,2},{4,5},{5,4},{6,7},{7,6},{8,9},{9,8},{10,11... | collective-permute-start | bytes 1769480 | tf_op jit(solution)/shard_map/ppermute | solution.py:374
  7.8 17.5 %copy-start.1 = (bf16[768,1536]{1,0:T(8,128)(2,1)S(1)}, bf16[768,1536]{1,0:T(8,128)(2,1)}, u32[]{:S(2)}) copy-start(bf16[768,1536]{1,0:T(8,128)(2,1)} %rest_10_.1) | copy-start | bytes 7077892
  7.8 17.5 %copy-start.3 = (bf16[128,1536]{1,0:T(8,128)(2,1)S(1)}, bf16[128,1536]{1,0:T(8,128)(2,1)}, u32[]{:S(2)}) copy-start(bf16[128,1536]{1,0:T(8,128)(2,1)} %embed_hbm.1) | copy-start | bytes 1179652
  7.8 17.5 %copy-start.4 = (bf16[1536,256]{1,0:T(8,128)(2,1)S(1)}, bf16[1536,256]{1,0:T(8,128)(2,1)}, u32[]{:S(2)}) copy-start(bf16[1536,256]{1,0:T(8,128)(2,1)} %head_hbm.1) | copy-start | bytes 2359300
  7.8 17.5 %copy-start.6 = (bf16[128,384]{1,0:T(8,128)(2,1)S(1)}, bf16[128,384]{1,0:T(8,128)(2,1)}, u32[]{:S(2)}) copy-start(bf16[128,384]{1,0:T(8,128)(2,1)} %copy-done.5) | copy-start | bytes 294916
  7.8 17.5 %copy-start.7 = (s32[8,3]{0,1:T(4,128)S(1)}, s32[8,3]{0,1:T(4,128)}, u32[]{:S(2)}) copy-start(s32[8,3]{0,1:T(4,128)} %param.11) | copy-start | bytes 292
  7.8 17.5 %copy-start.8 = (s32[8]{0:T(128)S(1)}, s32[8]{0:T(128)}, u32[]{:S(2)}) copy-start(s32[8]{0:T(128)} %frozen_ref.1) | copy-start | bytes 100
  9.0 7.5 %collective-permute-start.5 = (bf16[256,128]{1,0:T(8,128)(2,1)S(1)}, bf16[256,128]{1,0:T(8,128)(2,1)S(1)}, u32[]{:S(2)}, u32[]{:S(2)}) collective-permute-start(bf16[256,128]{1,0:T(8,128)(2,1)S(1)} %pick.1.rest_0_), channel_id=1, source_target_pairs={{0,12},{2,14},{4,8},{6,10},{8,4},{10,6},{12,0},{14,2},{1,13},{3,15... | collective-permute-start | bytes 196616 | tf_op jit(solution)/shard_map/ppermute | solution.py:378
  10.6 7.4 %collective-permute-start.3 = (bf16[256,128]{1,0:T(8,128)(2,1)S(1)}, bf16[256,128]{1,0:T(8,128)(2,1)S(1)}, u32[]{:S(2)}, u32[]{:S(2)}) collective-permute-start(bf16[256,128]{1,0:T(8,128)(2,1)S(1)} %pick.1.rest_0_), channel_id=1, source_target_pairs={{0,8},{2,10},{4,12},{6,14},{8,0},{10,2},{12,4},{14,6},{1,9},{3,11}... | collective-permute-start | bytes 196616 | tf_op jit(solution)/shard_map/ppermute | solution.py:378
  11.9 6.6 %collective-permute-start.1 = (bf16[256,128]{1,0:T(8,128)(2,1)S(1)}, bf16[256,128]{1,0:T(8,128)(2,1)S(1)}, u32[]{:S(2)}, u32[]{:S(2)}) collective-permute-start(bf16[256,128]{1,0:T(8,128)(2,1)S(1)} %pick.1.rest_0_), channel_id=1, source_target_pairs={{0,4},{2,6},{4,0},{6,2},{8,12},{10,14},{12,8},{14,10},{1,5},{3,7},... | collective-permute-start | bytes 196616 | tf_op jit(solution)/shard_map/ppermute | solution.py:378
  16.5 4.5 %collective-permute-start = (bf16[256,128]{1,0:T(8,128)(2,1)S(1)}, bf16[256,128]{1,0:T(8,128)(2,1)S(1)}, u32[]{:S(2)}, u32[]{:S(2)}) collective-permute-start(bf16[256,128]{1,0:T(8,128)(2,1)S(1)} %pick.1.rest_0_), channel_id=1, source_target_pairs={{0,2},{2,0},{4,6},{6,4},{8,10},{10,8},{12,14},{14,12},{1,3},{3,1},... | collective-permute-start | bytes 196616 | tf_op jit(solution)/shard_map/ppermute | solution.py:378
  18.0 5.0 %collective-permute-start.6 = (bf16[256,128]{1,0:T(8,128)(2,1)S(1)}, bf16[256,128]{1,0:T(8,128)(2,1)S(1)}, u32[]{:S(2)}, u32[]{:S(2)}) collective-permute-start(bf16[256,128]{1,0:T(8,128)(2,1)S(1)} %collective-permute-done.5.rest_6_), channel_id=1, source_target_pairs={{0,2},{2,0},{4,6},{6,4},{8,10},{10,8},{12,14},{14,12},{1,3},{3,1},... | collective-permute-start | bytes 196616 | tf_op jit(solution)/shard_map/ppermute | solution.py:378
  18.5 4.5 %collective-permute-start.4 = (bf16[256,128]{1,0:T(8,128)(2,1)S(1)}, bf16[256,128]{1,0:T(8,128)(2,1)S(1)}, u32[]{:S(2)}, u32[]{:S(2)}) collective-permute-start(bf16[256,128]{1,0:T(8,128)(2,1)S(1)} %collective-permute-done.3.rest_4_), channel_id=1, source_target_pairs={{0,2},{2,0},{4,6},{6,4},{8,10},{10,8},{12,14},{14,12},{1,3},{3,1},... | collective-permute-start | bytes 196616 | tf_op jit(solution)/shard_map/ppermute | solution.py:378
  21.0 4.3 %collective-permute-start.2 = (bf16[256,128]{1,0:T(8,128)(2,1)S(1)}, bf16[256,128]{1,0:T(8,128)(2,1)S(1)}, u32[]{:S(2)}, u32[]{:S(2)}) collective-permute-start(bf16[256,128]{1,0:T(8,128)(2,1)S(1)} %collective-permute-done.1.rest_2_), channel_id=1, source_target_pairs={{0,2},{2,0},{4,6},{6,4},{8,10},{10,8},{12,14},{14,12},{1,3},{3,1},... | collective-permute-start | bytes 196616 | tf_op jit(solution)/shard_map/ppermute | solution.py:378
